TPU v7x, 32 devices: a whole 2x2x4 slice. The times are simulated.
32 devices in a mesh: dp: 8 (over z, x), mp: 4 (over y, core).
Axes of the slice: x: 2, y: 2, z: 4, core: 2. Of those that a mesh axis runs over, the one named last changes fastest.
Arguments:
- patches: bfloat16 [32000, 768], P(('dp', 'mp')), may hold values from -6 to 6
- dataset_id: int32 [160], P('dp'), may hold values from 0 to 7
- patch_masks: int32 [8, 200], replicated, may hold values 0 or 1
- mask_tokens: bfloat16 [8, 768], replicated, may hold values from -6 to 6
- key_mask: int32 [160, 200], P('dp'), may hold values from 0 to 1, as said below
- bias_index: int32 [200, 200], replicated, may hold values from 0 to 731
- norm1_gain: float32 [768], replicated, may hold values from 0.5 to 1.5
- norm1_shift: float32 [768], replicated, may hold values from -1.8 to 1.8
- qkv_weight: bfloat16 [768, 3, 768], P(None, None, 'mp'), may hold values from -0.21875 to 0.21875
- query_bias: bfloat16 [768], P('mp'), may hold values from -3 to 3
- value_bias: bfloat16 [768], P('mp'), may hold values from -3 to 3
- bias_table: bfloat16 [732, 12], P(None, 'mp'), may hold values from -5 to 5
- out_weight: bfloat16 [768, 768], P('mp'), may hold values from -1.75 to 1.75
- out_bias: float32 [768], replicated, may hold values from -1.8 to 1.8
- gamma_attn: float32 [768], replicated, may hold values from 0.5 to 2
- norm2_gain: float32 [768], replicated, may hold values from 0.5 to 1.5
- norm2_shift: float32 [768], replicated, may hold values from -1.8 to 1.8
- up_weight: bfloat16 [768, 3072], P(None, 'mp'), may hold values from -0.21875 to 0.21875
- up_bias: bfloat16 [3072], P('mp'), may hold values from -3 to 3
- down_weight: bfloat16 [3072, 768], P('mp'), may hold values from -0.109375 to 0.109375
- down_bias: float32 [768], replicated, may hold values from -1.8 to 1.8
- gamma_mlp: float32 [768], replicated, may hold values from 0.5 to 2
- cotangent: bfloat16 [32000, 768], P(('dp', 'mp')), may hold values from -6 to 6
Outputs:
- output: bfloat16 [32000, 768], P(('dp', 'mp'))
- patch_grad: float32 [32000, 768], P(('dp', 'mp'))
- token_grad: float32 [8, 768], replicated
- norm1_gain_grad: float32 [768], replicated
- norm1_shift_grad: float32 [768], replicated
- qkv_grad: float32 [768, 3, 768], P(None, None, 'mp')
- query_bias_grad: float32 [768], P('mp')
- value_bias_grad: float32 [768], P('mp')
- table_grad: float32 [732, 12], P(None, 'mp')
- out_weight_grad: float32 [768, 768], P('mp')
- out_bias_grad: float32 [768], replicated
- gamma_attn_grad: float32 [768], replicated
- norm2_gain_grad: float32 [768], replicated
- norm2_shift_grad: float32 [768], replicated
- up_weight_grad: float32 [768, 3072], P(None, 'mp')
- up_bias_grad: float32 [3072], P('mp')
- down_weight_grad: float32 [3072, 768], P('mp')
- down_bias_grad: float32 [768], replicated
- gamma_mlp_grad: float32 [768], replicated
Inputs may be any that keep to these rules, and one draw needn't show every extreme that they name: `key_mask`: each row holds ones on a prefix of its positions and zeros after it; the first position is always one.
All inputs are finite; a program needn't handle non-finite values.
Results may differ from a plain program's by a relative error of at most 0.013.
The roundings to bfloat16 on the way count: a program that leaves them out, or rounds other values in their place, can miss the bound.
Values may be sent and summed in bfloat16 or wider, within the bound.
No kernel may reach another device: no remote copies, remote signals or barrier semaphores. Data moves between devices by JAX's collectives and lax.ppermute only.
A program may use at most 192 MiB of HBM per device.

v0:
```python
import jax
import jax.numpy as jnp
from jax import lax
from jax.sharding import PartitionSpec as P

HEAD = 64
SEQ = 200
GROUPS = 8
IMG_BLK = 5


def layer_norm(values, gain, shift):
    mean = jnp.mean(values, axis=-1, keepdims=True)
    centred = values - mean
    spread = jnp.mean(centred * centred, axis=-1, keepdims=True)
    return centred * lax.rsqrt(spread + 1e-06) * gain + shift


def gelu_exact(values):
    return jax.nn.gelu(values, approximate=False)


def product(left, right):
    return jnp.dot(left, right, preferred_element_type=jnp.float32)


def product_first(left, right):
    return lax.dot_general(
        left, right, (((0,), (0,)), ((), ())), preferred_element_type=jnp.float32
    )


def product_last(left, right):
    return lax.dot_general(
        left, right, (((1,), (1,)), ((), ())), preferred_element_type=jnp.float32
    )


def product_cross(left, right):
    return lax.dot_general(
        left, right, (((0,), (1,)), ((), ())), preferred_element_type=jnp.float32
    )


def score_block(queries, keys, bias, key_mask):
    scores = (
        jnp.einsum("bqhe,bkhe->bhqk", queries, keys, preferred_element_type=jnp.float32)
        + bias[None]
    )
    return jnp.where(key_mask[:, None, None, :] > 0, scores, -1e30)


def attention_forward(normed, qkv_all, qbias_all, vbias_all, table_all, masks_here, position_table):
    width = qkv_all.shape[2]
    heads = width // HEAD
    images = masks_here.shape[0]
    scale = HEAD ** (-0.5)
    joint = product(normed, qkv_all.reshape(qkv_all.shape[0], 3 * width))
    shape5 = (images // IMG_BLK, IMG_BLK, SEQ, heads, HEAD)
    queries = (
        ((joint[:, :width] + qbias_all.astype(jnp.float32)) * scale)
        .astype(jnp.bfloat16)
        .reshape(shape5)
    )
    keys = joint[:, width : 2 * width].astype(jnp.bfloat16).reshape(shape5)
    values = (
        (joint[:, 2 * width :] + vbias_all.astype(jnp.float32)).astype(jnp.bfloat16).reshape(shape5)
    )
    bias_flat = product_cross(table_all, position_table)
    bias = bias_flat.reshape(heads, SEQ, SEQ)
    block_masks = masks_here.reshape(images // IMG_BLK, IMG_BLK, SEQ)

    def attend(pieces):
        block_q, block_k, block_v, block_mask = pieces
        scores = score_block(block_q, block_k, bias, block_mask)
        largest = jnp.max(scores, axis=-1, keepdims=True)
        lse = largest + jnp.log(jnp.sum(jnp.exp(scores - largest), axis=-1, keepdims=True))
        probs = jnp.exp(scores - lse).astype(jnp.bfloat16)
        context = jnp.einsum("bhqk,bkhe->bqhe", probs, block_v, preferred_element_type=jnp.float32)
        return (context.astype(jnp.bfloat16), lse)

    context, lse = lax.map(attend, (queries, keys, values, block_masks))
    return (queries, keys, values, block_masks, bias, context.reshape(images * SEQ, width), lse)


def attention_backward(queries, keys, values, block_masks, bias, lse, grad_context, position_table):
    heads = queries.shape[3]
    width = heads * HEAD
    scale = HEAD ** (-0.5)
    grad_blocks = grad_context.reshape(queries.shape)

    def step(total, pieces):
        block_q, block_k, block_v, block_mask, block_lse, block_grad = pieces
        scores = score_block(block_q, block_k, bias, block_mask)
        probs = jnp.exp(scores - block_lse)
        grad_probs = jnp.einsum(
            "bqhe,bkhe->bhqk", block_grad, block_v, preferred_element_type=jnp.float32
        )
        centre = jnp.sum(probs * grad_probs, axis=-1, keepdims=True)
        grad_scores = (probs * (grad_probs - centre)).astype(jnp.bfloat16)
        grad_values = jnp.einsum(
            "bhqk,bqhe->bkhe",
            probs.astype(jnp.bfloat16),
            block_grad,
            preferred_element_type=jnp.float32,
        ).astype(jnp.bfloat16)
        grad_queries = (
            jnp.einsum(
                "bhqk,bkhe->bqhe", grad_scores, block_k, preferred_element_type=jnp.float32
            ).astype(jnp.bfloat16)
            * scale
        )
        grad_keys = jnp.einsum(
            "bhqk,bqhe->bkhe", grad_scores, block_q, preferred_element_type=jnp.float32
        ).astype(jnp.bfloat16)
        total = total + jnp.sum(grad_scores.astype(jnp.float32), axis=0)
        return (total, (grad_queries, grad_keys, grad_values))

    start_total = jnp.zeros((heads, SEQ, SEQ), jnp.float32)
    total, (grad_q, grad_k, grad_v) = lax.scan(
        step, start_total, (queries, keys, values, block_masks, lse, grad_blocks)
    )
    rows = grad_context.shape[0]
    grad_q = grad_q.reshape(rows, width)
    grad_k = grad_k.reshape(rows, width)
    grad_v = grad_v.reshape(rows, width)
    grad_joint = jnp.concatenate([grad_q, grad_k, grad_v], axis=1)
    qbias_local = jnp.sum(grad_q.astype(jnp.float32), axis=0)
    vbias_local = jnp.sum(grad_v.astype(jnp.float32), axis=0)
    total_flat = total.reshape(heads, SEQ * SEQ)
    upper_part = total_flat.astype(jnp.bfloat16)
    lower_part = (total_flat - upper_part.astype(jnp.float32)).astype(jnp.bfloat16)
    stacked = jnp.concatenate([upper_part, lower_part], axis=0)
    table_both = product_cross(position_table, stacked)
    table_local = table_both[:, :heads] + table_both[:, heads:]
    return (grad_joint, qbias_local, vbias_local, table_local)


def local(
    patches,
    dataset_id,
    patch_masks,
    mask_tokens,
    key_mask,
    bias_index,
    norm1_gain,
    norm1_shift,
    qkv_weight,
    query_bias,
    value_bias,
    bias_table,
    out_weight,
    out_bias,
    gamma_attn,
    norm2_gain,
    norm2_shift,
    up_weight,
    up_bias,
    down_weight,
    down_bias,
    gamma_mlp,
    cotangent,
):
    rows = patches.shape[0]
    mp_count = lax.axis_size("mp")
    mp_place = lax.axis_index("mp")
    images = dataset_id.shape[0]
    own_images = images // mp_count
    table_rows = bias_table.shape[0]
    own_ids = lax.dynamic_slice_in_dim(dataset_id, mp_place * own_images, own_images, 0)
    own_choose = (own_ids[:, None] == jnp.arange(GROUPS)[None, :]).astype(jnp.bfloat16)
    own_sel = product(own_choose, patch_masks.astype(jnp.bfloat16))
    selected = own_sel.reshape(rows, 1)
    row_choose = jnp.broadcast_to(own_choose[:, None, :], (own_images, SEQ, GROUPS)).reshape(
        rows, GROUPS
    )
    token_rows = jnp.broadcast_to(
        product(own_choose, mask_tokens)[:, None, :], (own_images, SEQ, mask_tokens.shape[1])
    ).reshape(rows, mask_tokens.shape[1])
    position_table = (bias_index.reshape(SEQ * SEQ, 1) == jnp.arange(table_rows)[None, :]).astype(
        jnp.bfloat16
    )
    start = patches.astype(jnp.float32) * (1.0 - selected) + selected * token_rows
    norm1_value, norm1_back = jax.vjp(layer_norm, start, norm1_gain, norm1_shift)
    normed1 = norm1_value.astype(jnp.bfloat16)
    attn_in = lax.all_gather(normed1, "mp", axis=0, tiled=True)
    qkv_all, qbias_all, vbias_all, table_all, out_all = (
        qkv_weight,
        query_bias,
        value_bias,
        bias_table,
        out_weight,
    )
    queries, keys, values, block_masks, bias, context, lse = attention_forward(
        attn_in, qkv_all, qbias_all, vbias_all, table_all, key_mask, position_table
    )
    out_part = product(context, out_all)
    attn_sum = lax.psum_scatter(out_part, "mp", scatter_dimension=0, tiled=True)
    attn_value = attn_sum + out_bias
    middle = start + gamma_attn * attn_value
    norm2_value, norm2_back = jax.vjp(layer_norm, middle, norm2_gain, norm2_shift)
    normed2 = norm2_value.astype(jnp.bfloat16)
    mlp_in = lax.all_gather(normed2, "mp", axis=0, tiled=True)
    up_all, upb_all, down_all = (up_weight, up_bias, down_weight)
    hidden_pre = product(mlp_in, up_all) + upb_all.astype(jnp.float32)
    hidden_act, gelu_back = jax.vjp(gelu_exact, hidden_pre)
    hidden = hidden_act.astype(jnp.bfloat16)
    down_part = product(hidden, down_all)
    mlp_sum = lax.psum_scatter(
        down_part.astype(jnp.bfloat16), "mp", scatter_dimension=0, tiled=True
    ).astype(jnp.float32)
    mlp_value = mlp_sum + down_bias
    output = (middle + gamma_mlp * mlp_value).astype(jnp.bfloat16)
    grad_out = cotangent.astype(jnp.float32)
    gamma_mlp_part = jnp.sum(grad_out * mlp_value, axis=0)
    grad_mlp = (gamma_mlp * grad_out).astype(jnp.bfloat16)
    down_bias_part = jnp.sum(grad_mlp.astype(jnp.float32), axis=0)
    grad_mlp_all = lax.all_gather(grad_mlp, "mp", axis=0, tiled=True)
    down_grad_local = product_first(hidden, grad_mlp_all)
    grad_hidden = product_last(grad_mlp_all, down_all)
    grad_pre = gelu_back(grad_hidden)[0].astype(jnp.bfloat16)
    up_bias_local = jnp.sum(grad_pre.astype(jnp.float32), axis=0)
    up_grad_local = product_first(mlp_in, grad_pre)
    norm2_part = product_last(grad_pre, up_all)
    grad_normed2 = lax.psum_scatter(norm2_part, "mp", scatter_dimension=0, tiled=True)
    up_grad, up_bias_grad, down_grad = (up_grad_local, up_bias_local, down_grad_local)
    grad_middle_norm, norm2_gain_part, norm2_shift_part = norm2_back(grad_normed2)
    grad_middle = grad_out + grad_middle_norm
    gamma_attn_part = jnp.sum(grad_middle * attn_value, axis=0)
    grad_attn = (gamma_attn * grad_middle).astype(jnp.bfloat16)
    out_bias_part = jnp.sum(grad_attn.astype(jnp.float32), axis=0)
    grad_attn_all = lax.all_gather(grad_attn, "mp", axis=0, tiled=True)
    out_grad_local = product_first(context, grad_attn_all)
    grad_context = product_last(grad_attn_all, out_all).astype(jnp.bfloat16)
    grad_joint, qbias_local, vbias_local, table_local = attention_backward(
        queries, keys, values, block_masks, bias, lse, grad_context, position_table
    )
    width = qkv_all.shape[2]
    model_width = qkv_all.shape[0]
    qkv_grad_local = product_first(attn_in, grad_joint).reshape(model_width, 3, width)
    norm1_part = product_last(grad_joint, qkv_all.reshape(model_width, 3 * width))
    grad_normed1 = lax.psum_scatter(
        norm1_part.astype(jnp.bfloat16), "mp", scatter_dimension=0, tiled=True
    ).astype(jnp.float32)
    qkv_grad, qbias_grad, vbias_grad, table_grad, out_grad = (
        qkv_grad_local,
        qbias_local,
        vbias_local,
        table_local,
        out_grad_local,
    )
    grad_start_norm, norm1_gain_part, norm1_shift_part = norm1_back(grad_normed1)
    grad_start = grad_middle + grad_start_norm
    patch_grad = grad_start * (1.0 - selected)
    token_part = lax.dot_general(
        row_choose.astype(jnp.float32),
        grad_start * selected,
        (((0,), (0,)), ((), ())),
        precision=lax.Precision.HIGHEST,
    )
    qkv_grad, qbias_grad, vbias_grad, table_grad, out_grad, up_grad, up_bias_grad, down_grad = (
        lax.psum(
            (
                qkv_grad,
                qbias_grad,
                vbias_grad,
                table_grad,
                out_grad,
                up_grad,
                up_bias_grad,
                down_grad,
            ),
            "dp",
        )
    )
    (
        token_grad,
        norm1_gain_grad,
        norm1_shift_grad,
        out_bias_grad,
        gamma_attn_grad,
        norm2_gain_grad,
        norm2_shift_grad,
        down_bias_grad,
        gamma_mlp_grad,
    ) = lax.psum(
        (
            token_part,
            norm1_gain_part,
            norm1_shift_part,
            out_bias_part,
            gamma_attn_part,
            norm2_gain_part,
            norm2_shift_part,
            down_bias_part,
            gamma_mlp_part,
        ),
        ("dp", "mp"),
    )
    return (
        output,
        patch_grad,
        token_grad,
        norm1_gain_grad,
        norm1_shift_grad,
        qkv_grad,
        qbias_grad,
        vbias_grad,
        table_grad,
        out_grad,
        out_bias_grad,
        gamma_attn_grad,
        norm2_gain_grad,
        norm2_shift_grad,
        up_grad,
        up_bias_grad,
        down_grad,
        down_bias_grad,
        gamma_mlp_grad,
    )


def solution(mesh):
    return jax.shard_map(
        local,
        mesh=mesh,
        in_specs=(
            P(("dp", "mp"), None),
            P("dp"),
            P(),
            P(),
            P("dp", None),
            P(),
            P(),
            P(),
            P(None, None, "mp"),
            P("mp"),
            P("mp"),
            P(None, "mp"),
            P("mp", None),
            P(),
            P(),
            P(),
            P(),
            P(None, "mp"),
            P("mp"),
            P("mp", None),
            P(),
            P(),
            P(("dp", "mp"), None),
        ),
        out_specs=(
            P(("dp", "mp"), None),
            P(("dp", "mp"), None),
            P(),
            P(),
            P(),
            P(None, None, "mp"),
            P("mp"),
            P("mp"),
            P(None, "mp"),
            P("mp", None),
            P(),
            P(),
            P(),
            P(),
            P(None, "mp"),
            P("mp"),
            P("mp", None),
            P(),
            P(),
        ),
        check_vma=False,
    )
```

profile of v0, /device:TPU:0, one launch (start us, length us, event | category | flops | bytes accessed | tf_op | source)
XLA Modules:
  0.0 1081.7 jit_solution(13086309809975984235)
XLA Ops:
  22.6 18.9 %fusion.61 = f32[3,40000]{1,0:T(4,128)} fusion(bf16[732,3]{0,1:T(4,128)(2,1)S(1)} %copy-done.62, s32[40000]{0:T(1024)S(1)} %eq.35), kind=kOutput, calls=%fused_computation.71 | convolution fusion | flops 204960000 | bytes 644392 | tf_op jit(solution)/shard_map/dot_general | solution.py:40
  44.3 26.1 %all-gather.5.cloned.1.call-done = bf16[4000,768]{1,0:T(8,128)(2,1)} async-done(((bf16[1000,768]{1,0:T(8,128)(2,1)}), bf16[4000,768]{1,0:T(8,128)(2,1)}) %all-gather.5.cloned.1.call-update) | async-done | bytes 6144016 | tf_op jit(solution)/shard_map/all_gather | solution.py:186
  92.3 7.6 reshape.239
  117.7 30.9 %while.31 = (s32[]{:T(128)}, bf16[4,5,200,3,64]{2,4,3,1,0:T(8,128)(2,1)}, f32[4,5,3,200,1]{3,2,1,4,0:T(4,128)}, bf16[4,5,200,3,64]{2,4,3,1,0:T(8,128)(2,1)}, s32...) while((s32[]{:T(128)}, ...), condition=%wide.wide.region_5.6_spmd, body=%wide.wide.region_2.5_spmd.sunk | while | flops 160390000 | bytes 11681225 | solution.py:82
  158.8 7.7 fusion.96
  166.7 97.1 %reduce-scatter.5.cloned.1.call-done = f32[1000,768]{1,0:T(8,128)} async-done(((f32[4000,768]{1,0:T(8,128)}), f32[1000,768]{1,0:T(8,128)}) %reduce-scatter.5.cloned.1.call-update) | async-done | bytes 3072016 | tf_op jit(solution)/shard_map/reduce_scatter | solution.py:198
  277.0 43.4 %all-gather.7.cloned.1.call-done = bf16[4000,768]{1,0:T(8,128)(2,1)} async-done(((bf16[1000,768]{1,0:T(8,128)(2,1)}), bf16[4000,768]{1,0:T(8,128)(2,1)}) %all-gather.7.cloned.1.call-update) | async-done | bytes 6144016 | tf_op jit(solution)/shard_map/all_gather | solution.py:203
  320.4 13.8 %fusion.97 = f32[4000,768]{1,0:T(8,128)} fusion(bf16[4000,768]{1,0:T(8,128)(2,1)} %all-gather.7.cloned.1.call-done, bf16[768,768]{1,0:T(8,128)(2,1)} %param.44), kind=kOutput, calls=%fused_computation.165 | convolution fusion | flops 4718592000 | bytes 19611648 | tf_op jit(solution)/shard_map/dot_general | solution.py:24
  334.2 33.8 %all-gather.9.cloned.1.call-done = bf16[4000,768]{1,0:T(8,128)(2,1)} async-done(((bf16[1000,768]{1,0:T(8,128)(2,1)}), bf16[4000,768]{1,0:T(8,128)(2,1)}) %all-gather.9.cloned.1.call-update) | async-done | bytes 6144016 | tf_op jit(solution)/shard_map/all_gather | solution.py:218
  368.0 36.0 %convert_reduce_fusion.1 = (f32[768]{0:T(1024)}, bf16[4000,768]{1,0:T(8,128)(2,1)S(1)}, f32[4000,768]{1,0:T(8,128)}) fusion(f32[4000,768]{1,0:T(8,128)} %fusion.97, f32[768]{0:T(1024)S(1)} %convert_element_type.138, bf16[4000,768]{1,0:T(8,128)(2,1)} %all-gather.9.cloned.1.call-done, bf16[768,768]{1,0:T(8,128)(2,1)S(1)} %copy-done), kind=kOutput, calls=%fused_computation.74 | convolution fusion | flops 4948990976 | bytes 38049792 | tf_op jit(solution)/shard_map/dot_general | solution.py:34
  406.5 7.9 fusion.98
  414.7 11.1 %multiply_convert_fusion.1 = bf16[4000,768]{1,0:T(8,128)(2,1)S(1)} fusion(f32[4000,768]{1,0:T(8,128)} %get-tuple-element.343, f32[4000,768]{1,0:T(8,128)} %fusion.97, f32[768]{0:T(1024)S(1)} %convert_element_type.138), kind=kLoop, calls=%fused_computation.76 | loop fusion | flops 12288000 | bytes 30723072 | tf_op jit(solution)/shard_map/convert_element_type | solution.py:207
  436.4 75.3 %reduce-scatter.9.cloned.1.call-done = f32[1000,768]{1,0:T(8,128)} async-done(((f32[4000,768]{1,0:T(8,128)}), f32[1000,768]{1,0:T(8,128)}) %reduce-scatter.9.cloned.1.call-update) | async-done | bytes 3072016 | tf_op jit(solution)/shard_map/reduce_scatter | solution.py:225
  514.6 56.9 %reduce-scatter.7.cloned.1.call-done = bf16[1000,768]{1,0:T(8,128)(2,1)} async-done(((bf16[4000,768]{1,0:T(8,128)(2,1)}), bf16[1000,768]{1,0:T(8,128)(2,1)}) %reduce-scatter.7.cloned.1.call-update) | async-done | bytes 1536016 | tf_op jit(solution)/shard_map/reduce_scatter | solution.py:209
  580.2 43.9 %all-gather.11.cloned.1.call-done = bf16[4000,768]{1,0:T(8,128)(2,1)} async-done(((bf16[1000,768]{1,0:T(8,128)(2,1)}), bf16[4000,768]{1,0:T(8,128)(2,1)}) %all-gather.11.cloned.1.call-update) | async-done | bytes 6144016 | tf_op jit(solution)/shard_map/all_gather | solution.py:232
  644.0 85.4 %while.32 = (s32[]{:T(128)}, f32[3,200,200]{1,2,0:T(8,128)}, bf16[4,5,200,3,64]{2,4,3,1,0:T(8,128)(2,1)}, bf16[4,5,200,3,64]{2,4,3,1,0:T(8,128)(2,1)}, bf16[4,5,...) while((s32[]{:T(128)}, f32[3,200,200]{1,2,0:T(8,128)}, ...), condition=%wide.wide.region_16.17_spmd.clone, body=%wide.wide.region_13.16_spmd.clone.sunk | while | flops 392062016 | bytes 36752904 | solution.py:120
  757.6 9.4 convolution_convert_fusion.2
  767.7 10.0 fusion.100
  777.7 10.6 fusion.101
  794.4 7.8 fusion.102
  806.3 23.4 %fusion.57 = f32[732,6]{0,1:T(8,128)S(1)} fusion(s32[40000]{0:T(1024)} %copy-done.36, bf16[3,40000]{1,0:T(4,128)(2,1)S(1)} %get-tuple-element.344, bf16[3,40000]{1,0:T(4,128)(2,1)} %get-tuple-element.345), kind=kOutput, calls=%fused_computation.67 | convolution fusion | flops 381600000 | bytes 657568 | tf_op jit(solution)/shard_map/dot_general | solution.py:40
  829.8 39.7 %all-reduce.1 = (f32[192]{0:T(256)}, f32[192]{0:T(256)}, f32[732,3]{0,1:T(4,128)}, f32[768]{0:T(1024)}) all-reduce(f32[192]{0:T(256)S(1)} %reduce_sum.245, f32[192]{0:T(256)S(1)} %reduce_sum.247, f32[732,3]{0,1:T(4,128)S(1)} %slice_add_fusion.2, f32[768]{0:T(1024)S(1)} %copy-done.55), channel_id=1, replica_groups=mesh['dp'=8,'mp'=4] {'dp'}, use_global_device_ids=true, to_apply=%region_27.28 | all-reduce | flops 3348 | bytes 26784 | tf_op jit(solution)/shard_map/psum | solution.py:262
  888.4 41.2 %all-reduce = (f32[8,768]{1,0:T(8,128)}, f32[768]{0:T(1024)}, f32[768]{0:T(1024)}, f32[768]{0:T(1024)}, f32[768]{0:T(1024)}, /*index=5*/f32[768]{0:T(1024)}, f32[768]{0:T(1024)}, f32[768]{0:T(1024)}, f32[768]{0:T(1024)}) all-reduce(f32[8,768]{1,0:T(8,128)S(1)} %fusion.77, ...), channel_id=1, replica_groups=mesh['dp'=8,'mp'=4] {'dp','mp'}, use_global_device_ids=true, to_apply=%region_20.21 | all-reduce | flops 12288 | bytes 98304 | tf_op jit(solution)/shard_map/psum | solution.py:286
  929.6 138.8 %all-reduce.5.cloned.1.call-done = (f32[768,3,192]{0,2,1:T(8,128)}, f32[192,768]{1,0:T(8,128)}, f32[768,768]{1,0:T(8,128)}, f32[768,768]{1,0:T(8,128)}) async-done(((f32[768,3,192]{0,2,1:T(8,128)}, f32[192,768]{1,0:T(8,128)}, f32[768,768]{1,0:T(8,128)}, f32[768,768]{1,0:T(8,128)}), (f32[768,3,192]{0,2,1:T(8,128)}, f32[192,768]{1,0:T(8,128)}, f32[768,768]{1,0:T(8,128)}, ...) | async-done | bytes 7077904 | tf_op jit(solution)/shard_map/psum | solution.py:262
  (306 shorter events, 306.4 us)
Async XLA Ops:
  7.2 360.8 %copy-start = (bf16[768,768]{1,0:T(8,128)(2,1)S(1)}, bf16[768,768]{1,0:T(8,128)(2,1)}, u32[]{:S(2)}) copy-start(bf16[768,768]{1,0:T(8,128)(2,1)} %param.46) | copy-start | bytes 3538948
  7.2 63.3 %all-gather.5.cloned.1.call-start = ((), (), s32[]{:S(2)}) async-start(), calls=%async_computation.4 | async-start | bytes 7680000 | tf_op jit(solution)/shard_map/all_gather | solution.py:186
  9.0 254.7 %copy-start.31 = (f32[1000]{0:T(1024)}, f32[1000]{0:T(1024)S(1)}, u32[]{:S(2)}) copy-start(f32[1000]{0:T(1024)S(1)} %reshape.234) | copy-start | bytes 12004
  9.0 254.7 %copy-start.34 = (f32[1000]{0:T(1024)}, f32[1000]{0:T(1024)S(1)}, u32[]{:S(2)}) copy-start(f32[1000]{0:T(1024)S(1)} %broadcast_subtract_fusion) | copy-start | bytes 12004
  10.0 253.8 %copy-start.25 = (f32[5,768]{1,0:T(8,128)}, f32[5,768]{1,0:T(8,128)S(1)}, u32[]{:S(2)}) copy-start(f32[5,768]{1,0:T(8,128)S(1)} %fusion.86) | copy-start | bytes 46084
  22.1 241.7 %reduce-scatter.5.cloned.1.call-start = ((), (), s32[]{:S(2)}) async-start(), calls=%async_computation.5 | async-start | bytes 15360000 | tf_op jit(solution)/shard_map/reduce_scatter | solution.py:198
  166.4 97.3 %copy-start.48 = (f32[768]{0:T(1024)S(1)}, f32[768]{0:T(1024)}, u32[]{:S(2)}) copy-start(f32[768]{0:T(1024)} %param.40) | copy-start | bytes 9220
  166.4 97.3 %copy-start.51 = (f32[768]{0:T(1024)S(1)}, f32[768]{0:T(1024)}, u32[]{:S(2)}) copy-start(f32[768]{0:T(1024)} %param.41) | copy-start | bytes 9220
  166.5 153.9 %all-gather.7.cloned.1.call-start = ((), (), s32[]{:S(2)}) async-start(), calls=%async_computation.6 | async-start | bytes 7680000 | tf_op jit(solution)/shard_map/all_gather | solution.py:203
  274.7 93.3 %all-gather.9.cloned.1.call-start = ((), (), s32[]{:S(2)}) async-start(), calls=%async_computation.8 | async-start | bytes 7680000 | tf_op jit(solution)/shard_map/all_gather | solution.py:218
  276.9 234.8 %reduce-scatter.9.cloned.1.call-start = ((), (), s32[]{:S(2)}) async-start(), calls=%async_computation.9 | async-start | bytes 15360000 | tf_op jit(solution)/shard_map/reduce_scatter | solution.py:225
  334.2 72.3 %copy-start.60 = (bf16[768,768]{1,0:T(8,128)(2,1)S(1)}, bf16[768,768]{1,0:T(8,128)(2,1)}, u32[]{:S(2)}) copy-start(bf16[768,768]{1,0:T(8,128)(2,1)} %param.44) | copy-start | bytes 3538948
  414.5 157.1 %reduce-scatter.7.cloned.1.call-start = ((), (), s32[]{:S(2)}) async-start(), calls=%async_computation.7 | async-start | bytes 7680000 | tf_op jit(solution)/shard_map/reduce_scatter | solution.py:209
  436.3 75.4 %copy-start.4 = (f32[1000,768]{1,0:T(8,128)S(1)}, f32[1000,768]{1,0:T(8,128)}, u32[]{:S(2)}) copy-start(f32[1000,768]{1,0:T(8,128)} %multiply_add_fusion) | copy-start | bytes 9216004
  436.3 135.2 %copy-start.50 = (f32[768]{0:T(1024)S(1)}, f32[768]{0:T(1024)}, u32[]{:S(2)}) copy-start(f32[768]{0:T(1024)} %param.47) | copy-start | bytes 9220
  436.3 187.7 %all-gather.11.cloned.1.call-start = ((), (), s32[]{:S(2)}) async-start(), calls=%async_computation.10 | async-start | bytes 7680000 | tf_op jit(solution)/shard_map/all_gather | solution.py:232
  578.4 291.1 %reduce-scatter.11.cloned.1.call-start = ((), (), s32[]{:S(2)}) async-start(), calls=%async_computation.11 | async-start | bytes 7680000 | tf_op jit(solution)/shard_map/reduce_scatter | solution.py:242
  767.0 301.4 %all-reduce.5.cloned.1.call-start = ((), (), s32[]{:S(2)}) async-start(), calls=%async_computation.12 | async-start | bytes 14155776 | tf_op jit(solution)/shard_map/psum | solution.py:262
  806.3 63.2 %copy-start.26 = (f32[5,768]{1,0:T(8,128)S(1)}, f32[5,768]{1,0:T(8,128)}, u32[]{:S(2)}) copy-start(f32[5,768]{1,0:T(8,128)} %copy-done.25) | copy-start | bytes 46084
  806.3 63.2 %copy-start.32 = (f32[1000]{0:T(1024)S(1)}, f32[1000]{0:T(1024)}, u32[]{:S(2)}) copy-start(f32[1000]{0:T(1024)} %copy-done.31) | copy-start | bytes 12004
  806.3 63.2 %copy-start.35 = (f32[1000]{0:T(1024)S(1)}, f32[1000]{0:T(1024)}, u32[]{:S(2)}) copy-start(f32[1000]{0:T(1024)} %copy-done.34) | copy-start | bytes 12004
  806.3 63.2 %copy-start.38 = (f32[1000]{0:T(1024)S(1)}, f32[1000]{0:T(1024)}, u32[]{:S(2)}) copy-start(f32[1000]{0:T(1024)} %copy-done.37) | copy-start | bytes 12004
  806.3 63.2 %copy-start.40 = (f32[1000]{0:T(1024)S(1)}, f32[1000]{0:T(1024)}, u32[]{:S(2)}) copy-start(f32[1000]{0:T(1024)} %copy-done.39) | copy-start | bytes 12004
  806.3 63.2 %copy-start.43 = (f32[768]{0:T(1024)S(1)}, f32[768]{0:T(1024)}, u32[]{:S(2)}) copy-start(f32[768]{0:T(1024)} %param.33) | copy-start | bytes 9220
  (56 other events, 429.3 us)
Sparse Core Ops, SparseCore 0:
  22.2 48.2 all-gather.4
  166.6 97.1 reduce-scatter.4
  274.8 45.5 all-gather.6
  322.4 45.5 all-gather.8
  414.6 97.0 reduce-scatter.8
  514.1 57.3 reduce-scatter.6
  578.5 45.5 all-gather.10
  767.1 57.3 reduce-scatter.10
  830.7 237.6 all-reduce.4
where the time goes:
time: 1090 us; the launch traced here: 1080 us
  waiting for transfers between devices  515 us (47%)
  matrix products  252 us (23%)
  local copies, waits for them, and re-layouts  130 us (12%)
  other arithmetic  87.4 us (8%)
  blocking collectives  80.9 us (7%)
  between operations  14.8 us (1%)
    psum x1, waiting for transfers between devices, local(): lax.psum((qkv_grad, qbias_grad, vbias_grad, table_grad, out_grad, up_grad...  139 us
    reduce_scatter x1, waiting for transfers between devices, local(): attn_sum = lax.psum_scatter(out_part, 'mp', scatter_dimension=0, tiled=True)  97.1 us
    reduce_scatter x1, waiting for transfers between devices, local(): lax.psum_scatter(norm2_part, 'mp', scatter_dimension=0, tiled=True)  75.3 us
    dot_general x4, matrix products, product_last(): lax.dot_general(left, right, (((1,), (1,)), ((), ())), preferred_element_...  59.3 us
    reduce_scatter x1, waiting for transfers between devices, local(): lax.psum_scatter(down_part.astype(jnp.bfloat16), 'mp', scatter_dimension=...  56.9 us
    all_gather x1, waiting for transfers between devices, local(): grad_attn_all = lax.all_gather(grad_attn, 'mp', axis=0, tiled=True)  43.9 us
    all_gather x1, waiting for transfers between devices, local(): mlp_in = lax.all_gather(normed2, 'mp', axis=0, tiled=True)  43.4 us
    dot_general x2, matrix products, product_cross(): lax.dot_general(left, right, (((0,), (1,)), ((), ())), preferred_element_...  42.3 us
  transfers between devices with their start and end apart: 9, of which 8 were waited for; matrix products, arithmetic and copies ran while one was open for 13% of the time, Pallas kernels for 0%

commit v1 on v0

v1 whole, which is shorter than its diff:
```python
import functools

import jax
import jax.numpy as jnp
from jax import lax
from jax.experimental import pallas as pl
from jax.experimental.pallas import tpu as pltpu
from jax.sharding import PartitionSpec as P

HEAD = 64
SEQ = 200
GROUPS = 8
LANES = 128
BF = jnp.bfloat16
F32 = jnp.float32
VMEM_LIMIT = 56 << 20


def dot_nn(left, right):
    return lax.dot_general(left, right, (((1,), (0,)), ((), ())), preferred_element_type=F32)


def dot_nt(left, right):
    return lax.dot_general(left, right, (((1,), (1,)), ((), ())), preferred_element_type=F32)


def dot_tn(left, right):
    return lax.dot_general(left, right, (((0,), (0,)), ((), ())), preferred_element_type=F32)


def params(steps=1):
    return pltpu.CompilerParams(
        dimension_semantics=("arbitrary",) * steps, vmem_limit_bytes=VMEM_LIMIT
    )


def cost(micros):
    return pl.CostEstimate(flops=int(micros * 1.1e8), transcendentals=0, bytes_accessed=0)


def whole(shape, at=0):
    zeros = (0,) * (len(shape) - 1)
    return pl.BlockSpec(shape, lambda *_: (at,) + zeros, pipeline_mode=pl.Buffered(1))


def image_spec(width):
    return pl.BlockSpec((1, SEQ, width), lambda i, *_: (i, 0, 0))


def resident(shape):
    zeros = (0,) * len(shape)
    return pl.BlockSpec(shape, lambda *_: zeros)


def shaped(shape, dtype):
    return jax.ShapeDtypeStruct(shape, dtype)


TILE = 40


def normalise(values):
    mean = jnp.mean(values, axis=-1, keepdims=True)
    centred = values - mean
    spread = jnp.mean(centred * centred, axis=-1, keepdims=True)
    scale = lax.rsqrt(spread + 1e-06)
    return centred * scale, scale


def normalise_back(grad, gain, xhat, scale):
    u = grad * gain
    return (
        u - jnp.mean(u, axis=-1, keepdims=True) - xhat * jnp.mean(u * xhat, axis=-1, keepdims=True)
    ) * scale


def line(ref):
    return ref[...].reshape(1, -1)


def token_line(ids_ref, token_ref):
    tokens = token_ref[...].astype(F32)
    group = lax.broadcasted_iota(jnp.int32, tokens.shape, 0)
    return jnp.sum(jnp.where(group == ids_ref[pl.program_id(0)], tokens, 0.0), axis=0, keepdims=True)


def mixed(patch_ref, sel_ref, token, at):
    sel = sel_ref[0, at : at + TILE, :]
    return patch_ref[0, at : at + TILE, :].astype(F32) * (1.0 - sel) + sel * token, sel


def tiles():
    return range(0, SEQ, TILE)


def fold(values):
    return jnp.sum(values.reshape(values.shape[0] // 8, 8, values.shape[1]), axis=0)


SMALL_ROWS = 16


def prepare_kernel(
    side_ref, qkv_ref, out_ref, down_ref, qb_ref, vb_ref, upb_ref, table_ref,
    small_ref, attn_ref, half_ref,
):
    own = qb_ref.shape[0]
    width = small_ref.shape[1]
    small_ref[...] = jnp.zeros_like(small_ref)
    small_ref[0:1, :own] = line(qb_ref)
    small_ref[0:1, 2 * own : 3 * own] = line(vb_ref)
    small_ref[1:2, : upb_ref.shape[0]] = line(upb_ref)
    small_ref[2 : 2 + table_ref.shape[0], : table_ref.shape[1]] = table_ref[...]
    attn_ref[2 * own :, :] = small_ref[...]

    @pl.when(side_ref[0] == 0)
    def _():
        attn_ref[: 2 * own, :] = qkv_ref[: 2 * own, :]
        half_ref[...] = down_ref[:, : width // 2]

    @pl.when(side_ref[0] == 1)
    def _():
        attn_ref[:own, :] = qkv_ref[2 * own :, :]
        attn_ref[own : 2 * own, :] = out_ref[...]
        half_ref[...] = down_ref[:, width // 2 :]


def prepare(side, qkv, out, down, qb, vb, upb, table):
    width = out.shape[1]
    vmem = pl.BlockSpec(memory_space=pltpu.VMEM)
    return pl.pallas_call(
        prepare_kernel,
        out_shape=[
            shaped((SMALL_ROWS, width), BF),
            shaped((2 * qb.shape[0] + SMALL_ROWS, width), BF),
            shaped((down.shape[0], width // 2), BF),
        ],
        in_specs=[pl.BlockSpec(memory_space=pltpu.SMEM)] + [vmem] * 7,
        out_specs=[vmem] * 3,
        compiler_params=pltpu.CompilerParams(vmem_limit_bytes=VMEM_LIMIT),
        cost_estimate=cost(2),
        name="prepare",
    )(side, qkv, out, down, qb, vb, upb, table)


def bias_kernel(near_ref, far_ref, index_ref, out_ref):
    own = out_ref.shape[0] // 2
    chunks = near_ref.shape[1] // LANES
    tables = (near_ref[...].astype(F32), far_ref[...].astype(F32))
    for row in range(0, SEQ, 8):
        for col in range(0, index_ref.shape[1], LANES):
            index = index_ref[row : row + 8, col : col + LANES]
            low = index & (LANES - 1)
            high = index >> 7
            for head in range(2 * own):
                table_ref, at = (0, 2 + head) if head < own else (1, 2 + head - own)
                found = jnp.zeros((8, LANES), F32)
                for chunk in range(chunks):
                    source = jnp.broadcast_to(
                        tables[table_ref][at : at + 1, chunk * LANES : (chunk + 1) * LANES], (8, LANES)
                    )
                    picked = jnp.take_along_axis(source, low, axis=1)
                    found = jnp.where(high == chunk, picked, found)
                out_ref[head, row : row + 8, col : col + LANES] = found


def small_spec(small):
    return whole((SMALL_ROWS, small[0].shape[1]), small[1])


def position_bias(small, heads, index):
    return pl.pallas_call(
        bias_kernel,
        out_shape=shaped((heads, SEQ, index.shape[1]), F32),
        grid=(1,),
        in_specs=[small_spec(item) for item in small] + [whole(index.shape)],
        out_specs=resident((heads, SEQ, index.shape[1])),
        compiler_params=pltpu.CompilerParams(vmem_limit_bytes=VMEM_LIMIT),
        cost_estimate=cost(4),
        name="position_bias",
    )(*[item for item, _ in small], index)


TABLE_ROWS = 8


def table_kernel(*refs):
    total_refs, (index_ref, out_ref) = refs[:4], refs[4:]

    @pl.when(pl.program_id(0) == 0)
    def _():
        out_ref[...] = jnp.zeros_like(out_ref)

    chunks = out_ref.shape[0] // sum(ref.shape[0] for ref in total_refs)
    spots = lax.broadcasted_iota(jnp.int32, (LANES, SEQ), 0)
    acc = jnp.zeros(out_ref.shape, F32)
    for row in range(TABLE_ROWS):
        index = index_ref[row : row + 1, :]
        hot = (spots == (index & (LANES - 1))).astype(F32).astype(BF)
        high = index >> 7
        total = jnp.concatenate([ref[:, row, :] for ref in total_refs], axis=0)
        parts = [jnp.where(high == chunk, total, 0.0) for chunk in range(chunks)]
        acc = acc + dot_nt(jnp.concatenate(parts, axis=0).astype(BF), hot)
    out_ref[...] += acc


def table_sums(totals, index, chunks, first, steps):
    heads = sum(total.shape[0] for total in totals)
    return pl.pallas_call(
        table_kernel,
        out_shape=shaped((chunks * heads, LANES), F32),
        grid=(steps,),
        in_specs=[
            pl.BlockSpec((total.shape[0], TABLE_ROWS, SEQ), lambda i: (0, first + i, 0))
            for total in totals
        ]
        + [pl.BlockSpec((TABLE_ROWS, SEQ), lambda i: (first + i, 0))],
        out_specs=resident((chunks * heads, LANES)),
        compiler_params=params(),
        cost_estimate=cost(8),
        name="table_sums",
    )(*totals, index)


def block(values, at):
    return values[:, at * LANES : (at + 1) * LANES]


def turned(values):
    return pltpu.roll(values, HEAD, 1)


def only(keep, values):
    return jnp.where(keep, values, jnp.zeros_like(values))


def lower_lanes():
    return lax.broadcasted_iota(jnp.int32, (SEQ, LANES), 1) < HEAD


def shard_forward(x, weight_ref, small_ref, bias_ref, mask, joint_ref, probs_ref, context_ref, base):
    width = joint_ref.shape[2]
    own = width // 3
    low = lower_lanes()
    high = jnp.logical_not(low)
    column = lax.broadcasted_iota(jnp.int32, (1, width), 1)
    scale = jnp.where(column < own, HEAD**-0.5, 1.0)
    joint = dot_nt(x, weight_ref[...])
    joint_ref[0] = ((joint + small_ref[...].astype(F32)[0:1, :width]) * scale).astype(BF)
    joint = joint_ref[0]
    b1, b2, b3 = block(joint, 1), block(joint, 2), block(joint, 3)
    t0, t1 = turned(block(joint, 0)), turned(b1)
    left = [only(high, b1), only(low, b2), only(high, b2)]
    right = [t0, t0, t1]
    value = [b3, b3, joint[:, 4 * LANES :]]
    found = []
    for head in range(3):
        scores = dot_nt(left[head], right[head]) + bias_ref[base + head][:, :SEQ] + mask
        raised = jnp.exp(scores - jnp.max(scores, axis=0, keepdims=True))
        probs = (raised * (1.0 / jnp.sum(raised, axis=0, keepdims=True))).astype(BF)
        probs_ref[0, base + head] = probs
        found.append(dot_tn(probs, value[head]))
    context_ref[0, :, :LANES] = jnp.where(low, found[0], found[1]).astype(BF)
    context_ref[0, :, LANES:] = found[2].astype(BF)


def attend_near_kernel(
    ids_ref, patch_ref, sel_ref, token_ref, gain_ref, shift_ref, w0_ref, w1_ref, s0_ref, s1_ref,
    o0_ref, o1_ref, bias_ref, mask_ref,
    normed_ref, joint0_ref, joint1_ref, probs_ref, context0_ref, context1_ref, part_ref,
):
    token = token_line(ids_ref, token_ref)
    for at in tiles():
        start, _ = mixed(patch_ref, sel_ref, token, at)
        xhat, _ = normalise(start)
        normed_ref[0, at : at + TILE, :] = (xhat * line(gain_ref) + line(shift_ref)).astype(BF)
    x = normed_ref[0]
    mask = mask_ref[0]
    own = w0_ref.shape[0] // 3 // HEAD
    shard_forward(x, w0_ref, s0_ref, bias_ref, mask, joint0_ref, probs_ref, context0_ref, 0)
    shard_forward(x, w1_ref, s1_ref, bias_ref, mask, joint1_ref, probs_ref, context1_ref, own)
    part_ref[0] = dot_nn(context0_ref[0], o0_ref[...]) + dot_nn(context1_ref[0], o1_ref[...])


def attend_far_kernel(
    ids_ref, side_ref, patch_ref, sel_ref, token_ref, normed_ref, part_ref, p0_ref, q0_ref, p1_ref,
    q1_ref, s0_ref, s1_ref, bias_ref, mask_ref, obias_ref, gamma_ref, gain_ref, shift_ref,
    joint0_ref, joint1_ref, probs_ref, context0_ref, context1_ref, value_ref, middle_ref, out_ref,
    pack0_ref, pack1_ref,
):
    half = p0_ref.shape[0] - SMALL_ROWS

    @pl.when(pl.program_id(0) == 0)
    def _():
        for side in range(2):
            @pl.when(side_ref[0] == side)
            def _():
                for p_ref, q_ref, pack_ref in ((p0_ref, q0_ref, pack0_ref), (p1_ref, q1_ref, pack1_ref)):
                    pack_ref[side * half : (side + 1) * half, :] = p_ref[:half, :]
                    pack_ref[(1 - side) * half : (2 - side) * half, :] = q_ref[:half, :]

    x = normed_ref[0]
    mask = mask_ref[0]
    joint = joint0_ref.shape[2]
    own = joint // 3 // HEAD
    w0_ref, w1_ref = pack0_ref.at[:joint], pack1_ref.at[:joint]
    o0_ref, o1_ref = pack0_ref.at[joint:], pack1_ref.at[joint:]
    shard_forward(x, w0_ref, s0_ref, bias_ref, mask, joint0_ref, probs_ref, context0_ref, 0)
    shard_forward(x, w1_ref, s1_ref, bias_ref, mask, joint1_ref, probs_ref, context1_ref, own)
    value_ref[0] = (
        dot_nn(context0_ref[0], o0_ref[...]) + dot_nn(context1_ref[0], o1_ref[...]) + part_ref[0]
    )
    token = token_line(ids_ref, token_ref)
    for at in tiles():
        rows = slice(at, at + TILE)
        start, _ = mixed(patch_ref, sel_ref, token, at)
        value = value_ref[0, rows, :] + line(obias_ref)
        middle = start + line(gamma_ref) * value
        xhat, _ = normalise(middle)
        value_ref[0, rows, :] = value
        middle_ref[0, rows, :] = middle
        out_ref[0, rows, :] = (xhat * line(gain_ref) + line(shift_ref)).astype(BF)


def mix_specs(width, groups):
    return [
        image_spec(width),
        pl.BlockSpec((1, SEQ, 1), lambda i, ids, *_: (ids[i], 0, 0)),
        whole((groups, width)),
    ]


def attend(mix, weights, smalls, bias, mask, before, after, first):
    ids, patches, sel_table, tokens = mix[-4:]
    images, _, width = patches.shape
    heads = bias.shape[0]
    joint = 3 * heads // 2 * HEAD
    context = joint // 3
    square = pl.BlockSpec((1, heads, SEQ, SEQ), lambda i, *_: (i, 0, 0, 0))
    rows = shaped(patches.shape, BF)
    wide = shaped(patches.shape, F32)
    per = shaped((images, SEQ, joint), BF)
    con = shaped((images, SEQ, context), BF)
    prob = shaped((images, heads, SEQ, SEQ), BF)
    small_specs = [small_spec(small) for small in smalls]
    smalls = [item for item, _ in smalls]
    position = [whole(bias.shape), image_spec(1)]
    core_out = [per, per, prob, con, con]
    core_spec = [image_spec(joint)] * 2 + [square] + [image_spec(context)] * 2
    vector = whole((width,))
    if first:
        w0, w1, o0, o1 = weights
        prefetch = [ids]
        in_specs = (
            [vector] * 2 + [whole((joint, width))] * 2 + small_specs + [whole((context, width))] * 2
            + position
        )
        operands = [*before, w0, w1, *smalls, o0, o1, bias, mask]
        out_shape = [rows] + core_out + [wide]
        out_specs = [image_spec(width)] + core_spec + [image_spec(width)]
        scratch = []
    else:
        prefetch = [ids, mix[0]]
        in_specs = (
            [image_spec(width)] * 2 + [whole(item.shape) for item in weights] + small_specs + position
            + [vector] * 4
        )
        operands = [*before, *weights, *smalls, bias, mask, *after]
        out_shape = core_out + [wide, wide, rows]
        out_specs = core_spec + [image_spec(width)] * 3
        scratch = [pltpu.VMEM((joint + context, width), BF)] * 2
        out_shape += [shaped((joint + context, width), BF)] * 2
        out_specs += [resident((joint + context, width))] * 2
        scratch = []
    return pl.pallas_call(
        attend_near_kernel if first else attend_far_kernel,
        out_shape=out_shape,
        grid_spec=pltpu.PrefetchScalarGridSpec(
            num_scalar_prefetch=len(prefetch),
            grid=(images,),
            in_specs=mix_specs(width, tokens.shape[0]) + in_specs,
            out_specs=out_specs,
            scratch_shapes=scratch,
        ),
        compiler_params=params(),
        cost_estimate=cost(19),
        name="attend_near" if first else "attend_far",
    )(*prefetch, patches, sel_table, tokens, *operands)


def shard_backward(
    x, grad, joint_ref, probs_ref, context_ref, weight_ref, out_ref, total_ref, sums_ref, acc_ref,
    joint_grad_ref, base,
):
    width = joint_ref.shape[2]
    own = width // 3
    low = lower_lanes()
    high = jnp.logical_not(low)
    grad_context = dot_nt(grad, out_ref[...]).astype(BF)
    d0, d1 = grad_context[:, :LANES], grad_context[:, LANES:]
    joint = joint_ref[0]
    b3 = block(joint, 3)
    t0, t1, t2 = turned(block(joint, 0)), turned(block(joint, 1)), turned(block(joint, 2))
    left = [only(low, b3), only(high, b3), joint[:, 4 * LANES :]]
    right = [d0, d0, d1]
    queries = [t0, t0, t1]
    keys = [t1, t2, t2]
    grads_q, grads_k, grads_v = [], [], []
    for head in range(3):
        probs = probs_ref[0, base + head]
        wide = probs.astype(F32)
        grad_probs = dot_nt(left[head], right[head])
        centre = jnp.sum(wide * grad_probs, axis=0, keepdims=True)
        grad_scores = (wide * (grad_probs - centre)).astype(BF)
        total_ref[base + head] += grad_scores.astype(F32)
        grads_v.append(dot_nn(probs, right[head]))
        grads_k.append(dot_nn(grad_scores, queries[head]))
        grads_q.append(dot_tn(grad_scores, keys[head]))
    scale = HEAD**-0.5
    blocks = [
        jnp.where(low, grads_q[0], grads_q[1]) * scale,
        jnp.where(low, grads_q[2] * scale, grads_k[0]),
        jnp.where(low, grads_k[1], grads_k[2]),
        jnp.where(low, grads_v[0], grads_v[1]),
        grads_v[2],
    ]
    for at, values in enumerate(blocks):
        cols = slice(at * LANES, at * LANES + values.shape[1])
        held = values.astype(BF)
        joint_grad_ref[:, cols] = held
        sums_ref[:, cols] += fold(held.astype(F32))
    joint_grad = joint_grad_ref[...]
    acc_ref[:width, :] += dot_tn(joint_grad, x)
    acc_ref[width:, :] += dot_tn(context_ref[0], grad)
    return dot_nn(joint_grad, weight_ref[...])


def attend_back_kernel(first, last, *refs):
    if last:
        ids_ref, patch_ref, sel_ref, token_ref, gmiddle_ref, gain_ref = refs[:6]
        refs = refs[6:]
    else:
        refs = refs[1:]
    if not first:
        carried_ref, refs = refs[0], refs[1:]
    x_ref, grad_ref, joint_ref, probs_ref, context_ref, weight_ref, out_ref = refs[:7]
    refs = refs[7:]
    g_ref, total_ref, sums_ref = refs[:3]
    refs = refs[3:]
    if last:
        patch_out_ref, norm_ref, token_out_ref, acc_ref, joint_grad_ref, carry_ref = refs
    else:
        carry_out_ref, acc_ref, joint_grad_ref = refs
    step = pl.program_id(0)

    @pl.when(step == 0)
    def _():
        for ref in (total_ref, sums_ref, acc_ref) + ((norm_ref,) if last else ()):
            ref[...] = jnp.zeros_like(ref)

    x = x_ref[0]
    part = shard_backward(
        x, grad_ref[0], joint_ref, probs_ref, context_ref, weight_ref, out_ref, total_ref, sums_ref,
        acc_ref, joint_grad_ref, 0,
    )
    if not first:
        part = part + carried_ref[0]
    if last:
        carry_ref[...] = part
        token = token_line(ids_ref, token_ref)
        token_sum = jnp.zeros((8, x.shape[1]), F32)
        for at in tiles():
            rows = slice(at, at + TILE)
            start, sel = mixed(patch_ref, sel_ref, token, at)
            xhat, scale = normalise(start)
            grad_normed = carry_ref[rows, :]
            norm_ref[0:8, :] += fold(grad_normed * xhat)
            norm_ref[8:16, :] += fold(grad_normed)
            grad_start = gmiddle_ref[0, rows, :] + normalise_back(
                grad_normed, line(gain_ref), xhat, scale
            )
            patch_out_ref[0, rows, :] = grad_start * (1.0 - sel)
            token_sum = token_sum + fold(grad_start * sel)
        token_out_ref[0] = token_sum
    else:
        carry_out_ref[0] = part

    @pl.when(step == pl.num_programs(0) - 1)
    def _():
        g_ref[...] = acc_ref[...].astype(BF)


def attend_back(ids, x, grad, joint, probs, turn, context, weight, out, carried, tail):
    images, _, width = x.shape
    joint_width = joint.shape[2]
    own = joint_width // 3
    heads = own // HEAD
    square = pl.BlockSpec((1, heads, SEQ, SEQ), lambda i, *_: (i, turn, 0, 0))
    first, last = carried is None, tail is not None
    in_specs = (
        [image_spec(width)] * 2
        + [image_spec(joint_width), square, image_spec(own)]
        + [whole((joint_width, width), weight[1]), whole((own, width), out[1])]
    )
    operands = [x, grad, joint, probs, context, weight[0], out[0]]
    if not first:
        in_specs = [image_spec(width)] + in_specs
        operands = [carried] + operands
    out_shape = [
        shaped((joint_width + own, width), BF),
        shaped((heads, SEQ, SEQ), F32),
        shaped((8, joint_width), F32),
    ]
    out_specs = [resident(item.shape) for item in out_shape]
    scratch = [pltpu.VMEM((joint_width + own, width), F32), pltpu.VMEM((SEQ, joint_width), BF)]
    if last:
        patches, sel_table, tokens, grad_middle, gain = tail
        in_specs = (
            mix_specs(width, tokens.shape[0]) + [image_spec(width), whole((width,))] + in_specs
        )
        operands = [patches, sel_table, tokens, grad_middle, gain] + operands
        out_shape += [
            shaped(x.shape, F32), shaped((16, width), F32), shaped((images, 8, width), F32)
        ]
        out_specs += [
            image_spec(width),
            resident((16, width)),
            pl.BlockSpec((1, 8, width), lambda i, *_: (i, 0, 0)),
        ]
        scratch.append(pltpu.VMEM((SEQ, width), F32))
    else:
        out_shape.append(shaped(x.shape, F32))
        out_specs.append(image_spec(width))
    return pl.pallas_call(
        functools.partial(attend_back_kernel, first, last),
        out_shape=out_shape,
        grid_spec=pltpu.PrefetchScalarGridSpec(
            num_scalar_prefetch=1,
            grid=(images,),
            in_specs=in_specs,
            out_specs=out_specs,
            scratch_shapes=scratch,
        ),
        compiler_params=params(),
        cost_estimate=cost(14),
        name="attend_back_last" if last else "attend_back",
    )(ids, *operands)


CHUNK = 256


def mlp_kernel(first, parted, *refs):
    if parted:
        side_ref, refs = refs[0], refs[1:]
    x_ref, cot_ref, gamma_ref, up_ref = refs[:4]
    refs = refs[4:]
    if parted:
        p_ref, q_ref = refs[:2]
        refs = refs[2:]
    else:
        down_ref = refs[0]
        refs = refs[1:]
    small_ref, refs = refs[0], refs[1:]
    if not first:
        value_in, grad_in = refs[:2]
        refs = refs[2:]
    value_ref, grad_ref, up_grad_ref, down_grad_ref, upb_grad_ref, gm_ref = refs[:6]
    step = pl.program_id(0)

    @pl.when(step == 0)
    def _():
        gm_ref[...] = (line(gamma_ref) * cot_ref[...].astype(F32)).astype(BF)
        if first:
            value_ref[...] = jnp.zeros_like(value_ref)
            grad_ref[...] = jnp.zeros_like(grad_ref)
        else:
            value_ref[...] = value_in[...]
            grad_ref[...] = grad_in[...]

    if parted:
        down_ref = refs[6]
        half = p_ref.shape[1]
        for side in range(2):
            @pl.when(side_ref[0] == side)
            def _():
                down_ref[:, side * half : (side + 1) * half] = p_ref[...]
                down_ref[:, (1 - side) * half : (2 - side) * half] = q_ref[...]

    x = x_ref[...]
    gm = gm_ref[...]
    up = up_ref[...]
    down = down_ref[...]
    before = dot_nn(x, up) + small_ref[...].astype(F32)[1:2, :]
    share = 0.5 + 0.5 * lax.erf(before * (0.5**0.5))
    density = jnp.exp(before * before * -0.5) * ((2.0 * jnp.pi) ** -0.5)
    hidden = (before * share).astype(BF)
    slope = share + before * density
    value_ref[...] += dot_nn(hidden, down)
    down_grad_ref[...] = dot_tn(hidden, gm).astype(BF)
    grad_before = (dot_nt(gm, down) * slope).astype(BF)
    upb_grad_ref[...] = fold(grad_before.astype(F32))
    up_grad_ref[...] = dot_tn(x, grad_before).astype(BF)
    grad_ref[...] += dot_nt(grad_before, up)


def mlp(x, cot, gamma, up, down, small, carried, side=None):
    rows, width = x.shape
    hidden = up.shape[1]
    parted = side is not None
    first = carried is None
    full = pl.BlockSpec((rows, width), lambda i, *_: (0, 0), pipeline_mode=pl.Buffered(1))
    up_spec = pl.BlockSpec((width, CHUNK), lambda i, *_: (0, i))
    down_spec = pl.BlockSpec((CHUNK, width), lambda i, *_: (i, 0))
    half_spec = pl.BlockSpec((CHUNK, width // 2), lambda i, *_: (i, 0))
    in_specs = [full, full, whole((width,)), up_spec]
    in_specs += [half_spec] * 2 if parted else [down_spec]
    in_specs += [pl.BlockSpec((SMALL_ROWS, CHUNK), lambda i, *_: (small[1], i))]
    operands = ([side] if parted else []) + [x, cot, gamma, up] + list(down) + [small[0]]
    aliases = {}
    if not first:
        aliases = {len(operands): 0, len(operands) + 1: 1}
        in_specs += [full, full]
        operands += list(carried)
    scratch = [pltpu.VMEM((rows, width), BF)]
    if parted:
        scratch.append(pltpu.VMEM((CHUNK, width), BF))
    return pl.pallas_call(
        functools.partial(mlp_kernel, first, parted),
        out_shape=(
            shaped((rows, width), F32),
            shaped((rows, width), F32),
            shaped((width, hidden), BF),
            shaped((hidden, width), BF),
            shaped((8, hidden), F32),
        ),
        grid_spec=pltpu.PrefetchScalarGridSpec(
            num_scalar_prefetch=1 if parted else 0,
            grid=(hidden // CHUNK,),
            in_specs=in_specs,
            out_specs=(
                full, full, up_spec, down_spec, pl.BlockSpec((8, CHUNK), lambda i, *_: (0, i))
            ),
            scratch_shapes=scratch,
        ),
        input_output_aliases=aliases,
        compiler_params=params(),
        cost_estimate=cost(16),
        name="mlp_far" if parted else "mlp_near",
    )(*operands)


def middle_back_kernel(
    value_ref, grad_ref, middle_ref, attn_ref, cot_ref, dbias_ref, gmlp_ref, gattn_ref, gain_ref,
    out_ref, gmiddle_ref, gattn_out_ref, sums_ref,
):
    @pl.when(pl.program_id(0) == 0)
    def _():
        sums_ref[...] = jnp.zeros_like(sums_ref)

    def add(row, values):
        sums_ref[8 * row : 8 * row + 8, :] += fold(values)

    for at in tiles():
        rows = slice(at, at + TILE)
        value = value_ref[0, rows, :] + line(dbias_ref)
        cot = cot_ref[0, rows, :].astype(F32)
        middle = middle_ref[0, rows, :]
        out_ref[0, rows, :] = (middle + line(gmlp_ref) * value).astype(BF)
        add(0, cot * value)
        add(1, (line(gmlp_ref) * cot).astype(BF).astype(F32))
        xhat, scale = normalise(middle)
        grad = grad_ref[0, rows, :]
        add(2, grad * xhat)
        add(3, grad)
        grad_middle = cot + normalise_back(grad, line(gain_ref), xhat, scale)
        gmiddle_ref[0, rows, :] = grad_middle
        add(4, grad_middle * attn_ref[0, rows, :])
        grad_attn = (line(gattn_ref) * grad_middle).astype(BF)
        gattn_out_ref[0, rows, :] = grad_attn
        add(5, grad_attn.astype(F32))


def middle_back(value, grad, middle, attn, cot, vectors):
    images, _, width = middle.shape
    return pl.pallas_call(
        middle_back_kernel,
        out_shape=(
            shaped(middle.shape, BF),
            shaped(middle.shape, F32),
            shaped(middle.shape, BF),
            shaped((48, width), F32),
        ),
        grid=(images,),
        in_specs=[image_spec(width)] * 5 + [whole((width,))] * 4,
        out_specs=(image_spec(width),) * 3 + (resident((48, width)),),
        compiler_params=params(),
        cost_estimate=cost(8),
        name="middle_back",
    )(value, grad, middle, attn, cot, *vectors)


def swap(values, axis, mask):
    count = lax.axis_size(axis)
    return lax.ppermute(values, axis, [(i, i ^ mask) for i in range(count)])


def dp_masks():
    count = lax.axis_size("dp")
    return [1 << bit for bit in range(count.bit_length() - 1)]


def pinned(value, *others):
    return lax.optimization_barrier((value,) + others)[0]


def plus(left, right):
    return (left.astype(F32) + right.astype(F32)).astype(BF)


ORDERS = ((0, 1), (1, 2))


def axis_bits():
    place = lax.axis_index("dp")
    return jnp.stack([(place >> bit) & 1 for bit in range(len(dp_masks()))]).astype(jnp.int32)


def halves_of(ref, base, size, bit):
    keep = pl.multiple_of(base + bit * size, 16)
    sent = pl.multiple_of(base + (1 - bit) * size, 16)
    return ref[pl.ds(keep, size), :], ref[pl.ds(sent, size), :]


def split_kernel(bits_ref, a_ref, b_ref, c_ref, *refs):
    outs, total_ref = refs[:4], refs[4]
    for at in range(0, total_ref.shape[0], 64):
        rows = slice(at, at + 64)
        total_ref[rows, :] = (
            a_ref[rows, :].astype(F32) + b_ref[rows, :].astype(F32) + c_ref[rows, :].astype(F32)
        ).astype(BF)
    part = total_ref.shape[0] // 2
    for which in range(2):
        keep, sent = halves_of(total_ref, which * part, part // 2, bits_ref[ORDERS[which][0]])
        outs[2 * which][...] = keep
        outs[2 * which + 1][...] = sent


def again_kernel(bits_ref, *refs):
    ins, outs, totals = refs[:4], refs[4:8], refs[8:]
    for which in range(2):
        total_ref = totals[which]
        total_ref[...] = plus(ins[2 * which][...], ins[2 * which + 1][...])
        size = total_ref.shape[0] // 2
        keep, sent = halves_of(total_ref, 0, size, bits_ref[ORDERS[which][1]])
        outs[2 * which][...] = keep
        outs[2 * which + 1][...] = sent


def both_kernel(bits_ref, *refs):
    for which in range(2):
        refs[4 + which][...] = plus(refs[2 * which][...], refs[2 * which + 1][...])


def put(out_ref, base, own, other, bit):
    size = own.shape[0]
    out_ref[pl.ds(pl.multiple_of(base + bit * size, 16), size), :] = own.astype(out_ref.dtype)
    out_ref[pl.ds(pl.multiple_of(base + (1 - bit) * size, 16), size), :] = other.astype(out_ref.dtype)


def grow_kernel(bits_ref, *refs):
    for which in range(2):
        put(refs[4 + which], 0, refs[2 * which][...], refs[2 * which + 1][...], bits_ref[ORDERS[which][1]])


def whole_kernel(bits_ref, *refs):
    ins, (first_ref, second_ref, total_ref) = refs[:4], refs[4:]
    part = total_ref.shape[0] // 2
    for which in range(2):
        put(total_ref, which * part, ins[2 * which][...], ins[2 * which + 1][...], bits_ref[ORDERS[which][0]])
    cut = first_ref.shape[0]
    first_ref[...] = total_ref[:cut, :].astype(F32)
    second_ref[...] = total_ref[cut:, :].astype(F32)


def step_call(kernel, bits, arrays, outs, scratch, name):
    vmem = pl.BlockSpec(memory_space=pltpu.VMEM)
    return pl.pallas_call(
        kernel,
        out_shape=outs,
        in_specs=[pl.BlockSpec(memory_space=pltpu.SMEM)] + [vmem] * len(arrays),
        out_specs=[vmem] * len(outs),
        scratch_shapes=scratch,
        compiler_params=pltpu.CompilerParams(vmem_limit_bytes=VMEM_LIMIT),
        cost_estimate=cost(1),
        name=name,
    )(bits, *arrays)


def dp_total(pieces, sizes, between):
    bits = axis_bits()
    masks = dp_masks()
    rows, width = pieces[0].shape
    quarter, eighth = shaped((rows // 4, width), BF), shaped((rows // 8, width), BF)

    def send(arrays, axes):
        got = [swap(array, "dp", masks[axis]) for array, axis in zip(arrays, axes)]
        between(got)
        return got

    a, a_sent, b, b_sent = step_call(
        split_kernel, bits, pieces, [quarter] * 4, [pltpu.VMEM((rows, width), BF)], "dp_split"
    )
    a_got, b_got = send([a_sent, b_sent], [ORDERS[0][0], ORDERS[1][0]])
    a, a_sent, b, b_sent = step_call(
        again_kernel, bits, [a, a_got, b, b_got], [eighth] * 4,
        [pltpu.VMEM((rows // 4, width), BF)] * 2, "dp_again",
    )
    a_got, b_got = send([a_sent, b_sent], [ORDERS[0][1], ORDERS[1][1]])
    rest = [[axis for axis in range(len(masks)) if axis not in order] for order in ORDERS]
    a, b = step_call(both_kernel, bits, [a, a_got, b, b_got], [eighth] * 2, [], "dp_both")
    for axes in zip(*rest):
        a_got, b_got = send([a, b], axes)
        a, b = step_call(both_kernel, bits, [a, a_got, b, b_got], [eighth] * 2, [], "dp_both")
    a_got, b_got = send([a, b], [ORDERS[0][1], ORDERS[1][1]])
    a, b = step_call(grow_kernel, bits, [a, a_got, b, b_got], [quarter] * 2, [], "dp_grow")
    a_got, b_got = send([a, b], [ORDERS[0][0], ORDERS[1][0]])
    return step_call(
        whole_kernel, bits, [a, a_got, b, b_got],
        [shaped((size, width), F32) for size in sizes], [pltpu.VMEM((rows, width), BF)], "dp_whole",
    )


def collect_kernel(ids_ref, sums2_ref, sums1_ref, tokens_ref, table0_ref, table1_ref, *refs):
    upb_refs, joint_refs, (out_ref, sent_ref) = refs[:4], refs[4:8], refs[8:]
    out_ref[...] = jnp.zeros_like(out_ref)
    sent_ref[...] = jnp.zeros_like(sent_ref)
    table = table0_ref[...] + table1_ref[...]

    def total(values):
        return jnp.sum(values, axis=0, keepdims=True)

    lines = [total(sums2_ref[8 * i : 8 * i + 8, :]) for i in range(6)]
    lines += [total(sums1_ref[8 * i : 8 * i + 8, :]) for i in range(2)]
    images = [total(tokens_ref[i]) for i in range(tokens_ref.shape[0])]
    for group in range(GROUPS):
        found = jnp.zeros_like(images[0])
        for at, values in enumerate(images):
            found = found + jnp.where(ids_ref[at] == group, values, 0.0)
        lines.append(found)
    for at, values in enumerate(lines):
        out_ref[8 + at : 9 + at, :] = values
        sent_ref[8 + at : 9 + at, :] = values
    hidden = upb_refs[0].shape[1]
    for which in range(4):
        ref = out_ref if which % 2 == 0 else sent_ref
        base = 0 if which < 2 else 24
        ref[base : base + 1, :hidden] = total(upb_refs[which][...])
        joint = total(joint_refs[which][...])
        ref[base + 1 : base + 2, : joint.shape[1]] = joint
        per = table.shape[0] // (out_ref.shape[1] // LANES)
        own = per // 4
        for chunk in range(out_ref.shape[1] // LANES):
            ref[base + 2 : base + 2 + own, chunk * LANES : (chunk + 1) * LANES] = table[
                chunk * per + which * own : chunk * per + (which + 1) * own, :
            ]


def collect(ids, sums2, sums1, tokens, tables, upbs, joints):
    width = sums2.shape[1]
    vmem = pl.BlockSpec(memory_space=pltpu.VMEM)
    return pl.pallas_call(
        collect_kernel,
        out_shape=(shaped((32, width), F32), shaped((32, width), F32)),
        in_specs=[pl.BlockSpec(memory_space=pltpu.SMEM)] + [vmem] * 13,
        out_specs=(vmem, vmem),
        cost_estimate=cost(1),
        name="collect",
    )(ids, sums2, sums1, tokens, *tables, *upbs, *joints)


def emit_kernel(held_ref, got_ref, *outs):
    own = outs[9].shape[0]
    value = held_ref[...] + got_ref[...]
    for at in range(8):
        outs[at][...] = value[8 + at : 9 + at, :].reshape(-1)
    outs[8][...] = value[16:24, :]
    outs[9][...] = value[1:2, :own].reshape(-1)
    outs[10][...] = value[1:2, 2 * own : 3 * own].reshape(-1)
    outs[11][...] = value[2 : 2 + outs[11].shape[0], : outs[11].shape[1]]
    outs[12][...] = value[0:1, : outs[12].shape[0]].reshape(-1)


def emit(held, got, own, table_shape, hidden):
    width = held.shape[1]
    return pl.pallas_call(
        emit_kernel,
        out_shape=[shaped((width,), F32)] * 8
        + [
            shaped((GROUPS, width), F32),
            shaped((own,), F32),
            shaped((own,), F32),
            shaped(table_shape, F32),
            shaped((hidden,), F32),
        ],
        cost_estimate=cost(1),
        name="emit",
    )(held, got)


def local(
    patches, dataset_id, patch_masks, mask_tokens, key_mask, bias_index, norm1_gain, norm1_shift,
    qkv_weight, query_bias, value_bias, bias_table, out_weight, out_bias, gamma_attn, norm2_gain,
    norm2_shift, up_weight, up_bias, down_weight, down_bias, gamma_mlp, cotangent,
):
    rows, width = patches.shape
    images = rows // SEQ
    place = lax.axis_index("mp")
    own = qkv_weight.shape[2]
    own_heads = own // HEAD
    table_rows = bias_table.shape[0]
    chunks = width // LANES
    hidden = up_weight.shape[1]

    ids = lax.dynamic_slice_in_dim(dataset_id, place * images, images, 0)
    keys_here = lax.dynamic_slice_in_dim(key_mask, place * images, images, 0)
    mask = jnp.where(keys_here > 0, 0.0, -1e30).astype(F32)[:, :, None]
    sel_table = patch_masks.astype(F32)[:, :, None]
    images3 = patches.reshape(images, SEQ, width)
    cot3 = cotangent.reshape(images, SEQ, width)
    index = bias_index.T
    index_wide = jnp.pad(index, ((0, 0), (0, 2 * LANES - SEQ)))
    mix = (ids, images3, sel_table, mask_tokens)

    parity = lax.axis_index("dp") & 1
    side = parity.reshape(1)
    qkv_own = qkv_weight.transpose(1, 2, 0).reshape(3 * own, width)
    small, attn_half, down_half = prepare(
        side, qkv_own, out_weight, down_weight, query_bias, value_bias, up_bias, bias_table.T
    )
    small0, small1 = (small, 0), (swap(small, "mp", 1), 0)
    attn_p2 = swap(attn_half, "mp", 2)
    down_p2 = swap(down_half, "mp", 2)
    qkv1, out1 = swap(qkv_own, "mp", 1), swap(out_weight, "mp", 1)
    bias_near = position_bias([small0, small1], 2 * own_heads, index_wide)
    up2 = swap(pinned(up_weight, bias_near), "mp", 2)
    up1, down1 = swap(up_weight, "mp", 1), swap(down_weight, "mp", 1)

    attn_p2, bias_near = lax.optimization_barrier((attn_p2, bias_near))
    attn_q2 = swap(attn_p2, "dp", 1)
    attn_p3 = swap(attn_p2, "mp", 1)
    small2, small3 = (attn_p2, 2 * own // SMALL_ROWS), (attn_p3, 2 * own // SMALL_ROWS)
    normed1, j0, j1, probs_near, c0, c1, part = attend(
        mix, [qkv_own, qkv1, out_weight, out1], [small0, small1], bias_near, mask,
        [norm1_gain, norm1_shift], [], True,
    )
    part, attn_q2, down_p2 = lax.optimization_barrier((part, attn_q2, down_p2))
    attn_q3 = swap(attn_q2, "mp", 1)
    bias_far = position_bias([small2, small3], 2 * own_heads, pinned(index_wide, part))
    down_q2 = swap(down_p2, "dp", 1)
    down_p3 = swap(down_p2, "mp", 1)
    j2, j3, probs_far, c2, c3, attn_value, middle, normed2, pack2, pack3 = attend(
        (side,) + mix, [attn_p2, attn_q2, attn_p3, attn_q3], [small2, small3], bias_far, mask,
        [normed1, part], [out_bias, gamma_attn, norm2_gain, norm2_shift], False,
    )
    normed2, up2, down_q2 = lax.optimization_barrier((normed2, up2, down_q2))
    up3 = swap(up2, "mp", 1)
    down_q3 = swap(down_q2, "mp", 1)

    flat2 = normed2.reshape(rows, width)
    value, grad2, up_g1, down_g1, upb1 = mlp(
        flat2, cotangent, gamma_mlp, up1, [down1], small1, None
    )
    up_r1, down_r1 = swap(up_g1, "mp", 1), swap(down_g1, "mp", 1)
    value, grad2, up_g3, down_g3, upb3 = mlp(
        flat2, cotangent, gamma_mlp, up3, [down_p3, down_q3], small3, (value, grad2), side
    )
    up_r3, down_r3 = swap(up_g3, "mp", 1), swap(down_g3, "mp", 1)
    value, grad2, up_g2, down_g2, upb2 = mlp(
        flat2, cotangent, gamma_mlp, up2, [down_p2, down_q2], small2, (value, grad2), side
    )
    up_far, down_far = plus(up_g2, up_r3), plus(down_g2, down_r3)
    flat2, up_far = lax.optimization_barrier((flat2, up_far))
    up_r2 = swap(up_far, "mp", 2)
    value, grad2, up_g0, down_g0, upb0 = mlp(
        flat2, cotangent, gamma_mlp, up_weight, [down_weight], small0, (value, grad2)
    )
    value, down_far = lax.optimization_barrier((value, down_far))
    down_r2 = swap(down_far, "mp", 2)

    shape3 = (images, SEQ, width)
    output, grad_middle, grad_attn, sums2 = middle_back(
        value.reshape(shape3), grad2.reshape(shape3), middle, attn_value, cot3,
        [down_bias, gamma_mlp, gamma_attn, norm2_gain],
    )

    g3, total3, js3, carried = attend_back(
        ids, normed1, grad_attn, j3, probs_far, 1, c3, (pack3, 0), (pack3, 3), None, None
    )
    r3 = swap(g3, "mp", 1)
    up_sum = (up_g0.astype(F32) + up_r1.astype(F32) + up_r2.astype(F32)).astype(BF)
    down_sum = (down_g0.astype(F32) + down_r1.astype(F32) + down_r2.astype(F32)).astype(BF)
    carried, up_sum, down_sum = lax.optimization_barrier((carried, up_sum, down_sum))
    up_sum, down_sum = lax.psum((up_sum, down_sum), "dp")
    g2, total2, js2, carried = attend_back(
        ids, normed1, grad_attn, j2, probs_far, 0, c2, (pack2, 0), (pack2, 3), carried, None
    )
    far = plus(g2, r3)
    carried, far = lax.optimization_barrier((carried, far))
    r2 = swap(far, "mp", 2)
    g1, total1, js1, carried = attend_back(
        ids, normed1, grad_attn, j1, probs_near, 1, c1, (qkv1, 0), (out1, 0), carried, None
    )
    r1 = swap(g1, "mp", 1)
    g0, total0, js0, patch_grad, sums1, token_images = attend_back(
        ids, normed1, grad_attn, j0, probs_near, 0, c0, (qkv_own, 0), (out_weight, 0), carried,
        (images3, sel_table, mask_tokens, grad_middle, norm1_gain),
    )
    totals = [total0, total1, total2, total3]
    blocks = SEQ // TABLE_ROWS
    tables = []

    def between(got):
        nonlocal index
        if len(tables) < 2:
            first = len(tables) * (blocks // 2)
            steps = blocks // 2 if not tables else blocks - blocks // 2
            tables.append(table_sums(totals, index, chunks, first, steps))

    qkv_sum, out_sum = dp_total([g0, r1, r2], [3 * own, own], between)

    held, sent = collect(
        ids, sums2, sums1, token_images, tables, [upb0, upb1, upb2, upb3], [js0, js1, js2, js3]
    )
    held = held + swap(sent, "mp", 1)
    sent = jnp.concatenate([held[24:], held[8:24]], axis=0)
    held = held[:24] + swap(sent, "mp", 2)
    masks = dp_masks()
    for shift in masks[:-1]:
        held = held + swap(held, "dp", shift)
    (
        gamma_mlp_grad, down_bias_grad, gain2_grad, shift2_grad, gamma_attn_grad, out_bias_grad,
        gain1_grad, shift1_grad, token_grad, qb_grad, vb_grad, table_grad, upb_grad,
    ) = emit(held, swap(held, "dp", masks[-1]), own, (own_heads, table_rows), hidden)

    return (
        output.reshape(rows, width),
        patch_grad.reshape(rows, width),
        token_grad,
        gain1_grad,
        shift1_grad,
        qkv_sum.reshape(3, own, width).transpose(2, 0, 1),
        qb_grad,
        vb_grad,
        table_grad.T,
        out_sum,
        out_bias_grad,
        gamma_attn_grad,
        gain2_grad,
        shift2_grad,
        up_sum.astype(F32),
        upb_grad,
        down_sum.astype(F32),
        down_bias_grad,
        gamma_mlp_grad,
    )


def solution(mesh):
    return jax.shard_map(
        local,
        mesh=mesh,
        in_specs=(
            P(("dp", "mp"), None), P("dp"), P(), P(), P("dp", None), P(), P(), P(),
            P(None, None, "mp"), P("mp"), P("mp"), P(None, "mp"), P("mp", None), P(), P(), P(), P(),
            P(None, "mp"), P("mp"), P("mp", None), P(), P(), P(("dp", "mp"), None),
        ),
        out_specs=(
            P(("dp", "mp"), None), P(("dp", "mp"), None), P(), P(), P(), P(None, None, "mp"),
            P("mp"), P("mp"), P(None, "mp"), P("mp", None), P(), P(), P(), P(), P(None, "mp"),
            P("mp"), P("mp", None), P(), P(),
        ),
        check_vma=False,
    )
```

time: 1090 us -> 380 us (0.35)
  waiting for transfers between devices: 515 us -> 59.5 us
  matrix products: 252 us -> 0 us
  Pallas kernels: 0 us -> 228 us
  local copies, waits for them, and re-layouts: 130 us -> 16.1 us
  blocking collectives: 80.9 us -> 0 us
  other arithmetic: 87.4 us -> 14.8 us
  starting transfers between devices: 0.93 us -> 41.6 us
    dot_general x45 -> x0, matrix products: 252 us -> none  [the longest x4 59.3 us: product_last(): lax.dot_general(left, right, (((1,), (1,)), ((), ())), preferred_element_...]
    reduce_scatter x4 -> x0, waiting for transfers between devices: 229 us -> none  [the longest x1 97.1 us: local(): attn_sum = lax.psum_scatter(out_part, 'mp', scatter_dimension=0, tiled=True)]
    pallas_call x0 -> x24, Pallas kernels: none -> 228 us  [the longest x4 69.9 us: mlp(): pl.pallas_call(functools.partial(mlp_kernel, first, parted), out_shape=(s...]
    all_gather x4 -> x0, waiting for transfers between devices: 147 us -> none  [the longest x1 43.9 us: local(): grad_attn_all = lax.all_gather(grad_attn, 'mp', axis=0, tiled=True)]
    psum x1, waiting for transfers between devices: 139 us -> 0.01 us  [local(): up_sum, down_sum = lax.psum((up_sum, down_sum), 'dp')]
    psum x2 -> x0, blocking collectives: 80.9 us -> none  [the longest x1 41.2 us: local(): lax.psum((token_part, norm1_gain_part, norm1_shift_part, out_bias_part, g...]
    ppermute x0 -> x39, waiting for transfers between devices: none -> 59.5 us  [swap(): return lax.ppermute(values, axis, [(i, i ^ mask) for i in range(count)])]
    reshape x11 -> x0, local copies, waits for them, and re-layouts: 49.2 us -> none  [the longest x1 7.64 us: attention_forward(): queries = ((joint[:, :width] + qbias_all.astype(jnp.float32)) * scale).as...]
  transfers between devices with their start and end apart: 9 -> 40, of which waited for: 8 -> 11; matrix products, arithmetic and copies ran while one was open for 13% -> 3% of each run, Pallas kernels for 0% -> 51%
where the time goes in v1:
time: 380 us; the launch traced here: 375 us
  Pallas kernels  228 us (60%)
  waiting for transfers between devices  59.5 us (16%)
  starting transfers between devices  41.6 us (11%)
  local copies, waits for them, and re-layouts  16.1 us (4%)
  other arithmetic  14.8 us (4%)
  between operations  14.7 us (4%)
    pallas_call x4, Pallas kernels, mlp(): pl.pallas_call(functools.partial(mlp_kernel, first, parted), out_shape=(s...  69.9 us
    pallas_call x4, Pallas kernels, attend_back(): pl.pallas_call(functools.partial(attend_back_kernel, first, last), out_sh...  62.6 us
    ppermute x39, waiting for transfers between devices, swap(): return lax.ppermute(values, axis, [(i, i ^ mask) for i in range(count)])  59.5 us
    ppermute x39, starting transfers between devices, swap(): return lax.ppermute(values, axis, [(i, i ^ mask) for i in range(count)])  41.6 us
    pallas_call x2, Pallas kernels, attend(): pl.pallas_call(attend_near_kernel if first else attend_far_kernel, out_sh...  39.3 us
    pallas_call x2, Pallas kernels, table_sums(): pl.pallas_call(table_kernel, out_shape=shaped((chunks * heads, LANES), F3...  17 us
    pallas_call x6, Pallas kernels, step_call(): pl.pallas_call(kernel, out_shape=outs, in_specs=[pl.BlockSpec(memory_spac...  14.4 us
    unnamed x71, local copies, waits for them, and re-layouts  12.6 us
  transfers between devices with their start and end apart: 40, of which 11 were waited for; matrix products, arithmetic and copies ran while one was open for 3% of the time, Pallas kernels for 51%

profile of v1, /device:TPU:0, one launch (start us, length us, event | category | flops | bytes accessed | tf_op | source)
XLA Modules:
  0.0 375.0 jit_solution(8827086730729117199)
XLA Ops:
  16.0 4.1 %position_bias.2.bias_ref = f32[6,200,256]{2,1,0:T(8,128)} custom-call(bf16[16,768]{1,0:T(8,128)(2,1)} %get-tuple-element.131.near_ref.s0_ref.refs_5_, bf16[16,768]{1,0:T(8,128)(2,1)} %copy-done.33, s32[200,256]{1,0:T(8,128)} %pad.4.index_ref), custom_call_target="tpu_custom_call" | custom-call | flops 440000000 | tf_op jit(solution)/shard_map/position_bias/pallas_call | solution.py:172
  20.1 7.0 %collective-permute-done.3.near_ref.p0_ref.s0_ref.refs_7_ = bf16[400,768]{1,0:T(8,128)(2,1)S(1)} collective-permute-done((bf16[400,768]{1,0:T(8,128)(2,1)}, bf16[400,768]{1,0:T(8,128)(2,1)S(1)}, u32[]{:S(2)}, u32[]{:S(2)}) %collective-permute-start.3) | collective-permute-done | bytes 614432 | tf_op jit(solution)/shard_map/ppermute | solution.py:705
  35.2 18.9 %attend_near.1 = (bf16[5,200,768]{2,1,0:T(8,128)(2,1)}, bf16[5,200,576]{2,1,0:T(8,128)(2,1)}, bf16[5,200,576]{2,1,0:T(8,128)(2,1)}, bf16[5,6,200,200]{3,2,1,0:T(...) custom-call(s32[5]{0:T(128)} %dynamic_slice.6.ids_ref.refs_0_, ...), custom_call_target="tpu_custom_call" | custom-call | flops 2090000000 | tf_op jit(solution)/shard_map/attend_near/pallas_call | solution.py:375
  55.7 4.1 %position_bias.3.bias_ref = f32[6,200,256]{2,1,0:T(8,128)} custom-call(bf16[400,768]{1,0:T(8,128)(2,1)} %copy-done, bf16[400,768]{1,0:T(8,128)(2,1)} %copy-done.1, s32[200,256]{1,0:T(8,128)} %pad.4.index_ref), custom_call_target="tpu_custom_call" | custom-call | flops 440000000 | tf_op jit(solution)/shard_map/position_bias/pallas_call | solution.py:172
  60.6 20.3 %attend_far.1 = (bf16[5,200,576]{2,1,0:T(8,128)(2,1)}, bf16[5,200,576]{2,1,0:T(8,128)(2,1)}, bf16[5,6,200,200]{3,2,1,0:T(8,128)(2,1)}, bf16[5,200,192]{2,1,0:T(8...) custom-call(s32[5]{0:T(128)} %dynamic_slice.6.ids_ref.refs_0_, ...), custom_call_target="tpu_custom_call" | custom-call | flops 2090000000 | tf_op jit(solution)/shard_map/attend_far/pallas_call | solution.py:375
  83.1 15.6 %mlp_near.2 = (f32[1000,768]{1,0:T(8,128)}, f32[1000,768]{1,0:T(8,128)}, bf16[768,768]{1,0:T(8,128)(2,1)}, bf16[768,768]{1,0:T(8,128)(2,1)}, f32[8,768]{1,0:T(8,128)}) custom-call(bf16[1000,768]{1,0:T(8,128)(2,1)} %bitcast.27, bf16[1000,768]{1,0:T(8,128)(2,1)} %refs_1_.3, f32[768]{0:T(1024)} %gmlp_ref.1, bf16[768,768]{1,0:T(8,128)(2,1)} %copy-done.31, ...), custom_call_target="tpu_custom_call" | custom-call | flops 1760000000 | tf_op jit(solution)/shard_map/mlp_near/pallas_call | solution.py:628
  100.1 18.5 %mlp_far.2 = (f32[1000,768]{1,0:T(8,128)}, f32[1000,768]{1,0:T(8,128)}, bf16[768,768]{1,0:T(8,128)(2,1)}, bf16[768,768]{1,0:T(8,128)(2,1)}, f32[8,768]{1,0:T(8,128)}) custom-call(s32[1]{0:T(128)} %bitcast.side_ref.refs_0_, bf16[1000,768]{1,0:T(8,128)(2,1)} %bitcast.28, bf16[1000,768]{1,0:T(8,128)(2,1)} %refs_1_.3, ...), custom_call_target="tpu_custom_call", output_to_operand_aliasing={{0}: (8, {}), {1}: (9, {})} | custom-call | flops 1760000000 | tf_op jit(solution)/shard_map/mlp_far/pallas_call | solution.py:628
  119.3 18.3 %mlp_far.3 = (f32[1000,768]{1,0:T(8,128)}, f32[1000,768]{1,0:T(8,128)}, bf16[768,768]{1,0:T(8,128)(2,1)}, bf16[768,768]{1,0:T(8,128)(2,1)}, f32[8,768]{1,0:T(8,128)}) custom-call(s32[1]{0:T(128)} %bitcast.side_ref.refs_0_, bf16[1000,768]{1,0:T(8,128)(2,1)} %bitcast.29, bf16[1000,768]{1,0:T(8,128)(2,1)} %refs_1_.3, ...), custom_call_target="tpu_custom_call", output_to_operand_aliasing={{0}: (8, {}), {1}: (9, {})} | custom-call | flops 1760000000 | tf_op jit(solution)/shard_map/mlp_far/pallas_call | solution.py:628
  141.8 17.5 %mlp_near.3 = (f32[1000,768]{1,0:T(8,128)}, f32[1000,768]{1,0:T(8,128)}, bf16[768,768]{1,0:T(8,128)(2,1)}, bf16[768,768]{1,0:T(8,128)(2,1)}, f32[8,768]{1,0:T(8,128)}) custom-call(bf16[1000,768]{1,0:T(8,128)(2,1)} %bitcast.30, bf16[1000,768]{1,0:T(8,128)(2,1)} %refs_1_.3, f32[768]{0:T(1024)} %gmlp_ref.1, ...), custom_call_target="tpu_custom_call", output_to_operand_aliasing={{0}: (6, {}), {1}: (7, {})} | custom-call | flops 1760000000 | tf_op jit(solution)/shard_map/mlp_near/pallas_call | solution.py:628
  159.7 10.5 %middle_back.1 = (bf16[5,200,768]{2,1,0:T(8,128)(2,1)}, f32[5,200,768]{2,1,0:T(8,128)}, bf16[5,200,768]{2,1,0:T(8,128)(2,1)}, f32[48,768]{1,0:T(8,128)}) custom-call(f32[5,200,768]{2,1,0:T(8,128)} %bitcast.24, f32[5,200,768]{2,1,0:T(8,128)} %bitcast.25, f32[5,200,768]{2,1,0:T(8,128)} %get-tuple-element.161.middle_ref, ...), custom_call_target="tpu_custom_call" | custom-call | flops 880000000 | tf_op jit(solution)/shard_map/middle_back/pallas_call | solution.py:686
  170.2 15.1 %attend_back.3 = (bf16[768,768]{1,0:T(8,128)(2,1)}, f32[3,200,200]{2,1,0:T(8,128)}, f32[8,576]{1,0:T(8,128)}, f32[5,200,768]{2,1,0:T(8,128)}) custom-call(s32[5]{0:T(128)} %dynamic_slice.6.ids_ref.refs_0_, bf16[5,200,768]{2,1,0:T(8,128)(2,1)} %get-tuple-element.134.normed_ref.refs_1_.refs_2_.refs_7_, ...), custom_call_target="tpu_custom_call" | custom-call | flops 1540000000 | tf_op jit(solution)/shard_map/attend_back/pallas_call | solution.py:534
  186.8 6.7 %collective-permute-done.20 = bf16[768,768]{1,0:T(8,128)(2,1)} collective-permute-done((bf16[768,768]{1,0:T(8,128)(2,1)S(1)}, bf16[768,768]{1,0:T(8,128)(2,1)}, u32[]{:S(2)}, u32[]{:S(2)}) %collective-permute-start.20) | collective-permute-done | bytes 1179680 | tf_op jit(solution)/shard_map/ppermute | solution.py:705
  196.3 15.2 %attend_back.4 = (bf16[768,768]{1,0:T(8,128)(2,1)}, f32[3,200,200]{2,1,0:T(8,128)}, f32[8,576]{1,0:T(8,128)}, f32[5,200,768]{2,1,0:T(8,128)}) custom-call(s32[5]{0:T(128)} %dynamic_slice.6.ids_ref.refs_0_, f32[5,200,768]{2,1,0:T(8,128)} %get-tuple-element.177.refs_1_, bf16[5,200,768]{2,1,0:T(8,128)(2,1)} %get-tuple-element.134.normed_ref.refs_1_.refs_2_.refs_7_, ...), custom_call_target="tpu_custom_call" | custom-call | flops 1540000000 | tf_op jit(solution)/shard_map/attend_back/pallas_call | solution.py:534
  213.0 15.2 %attend_back.5 = (bf16[768,768]{1,0:T(8,128)(2,1)}, f32[3,200,200]{2,1,0:T(8,128)}, f32[8,576]{1,0:T(8,128)}, f32[5,200,768]{2,1,0:T(8,128)}) custom-call(s32[5]{0:T(128)} %dynamic_slice.6.ids_ref.refs_0_, f32[5,200,768]{2,1,0:T(8,128)} %get-tuple-element.184.refs_1_, bf16[5,200,768]{2,1,0:T(8,128)(2,1)} %get-tuple-element.134.normed_ref.refs_1_.refs_2_.refs_7_, ...), custom_call_target="tpu_custom_call" | custom-call | flops 1540000000 | tf_op jit(solution)/shard_map/attend_back/pallas_call | solution.py:534
  230.7 17.2 %attend_back_last.1 = (bf16[768,768]{1,0:T(8,128)(2,1)}, f32[3,200,200]{2,1,0:T(8,128)}, f32[8,576]{1,0:T(8,128)}, f32[5,200,768]{2,1,0:T(8,128)}, f32[16,768]{1,0:T(8,128)}, /*index=5*/f32[5,8,768]{2,1,0:T(8,128)}) custom-call(s32[5]{0:T(128)} %dynamic_slice.6.ids_ref.refs_0_, bf16[5,200,768]{2,1,0:T(8,128)(2,1)} %bitcast.33, ...), custom_call_target="tpu_custom_call" | custom-call | flops 1540000000 | tf_op jit(solution)/shard_map/attend_back_last/pallas_call | solution.py:534
  247.9 8.7 %collective-permute-done.28.c_ref = bf16[768,768]{1,0:T(8,128)(2,1)S(1)} collective-permute-done((bf16[768,768]{1,0:T(8,128)(2,1)S(1)}, bf16[768,768]{1,0:T(8,128)(2,1)S(1)}, u32[]{:S(2)}, u32[]{:S(2)}) %collective-permute-start.28) | collective-permute-done | bytes 1179680 | tf_op jit(solution)/shard_map/ppermute | solution.py:705
  264.5 5.6 %collective-permute-done.29.refs_1_ = bf16[192,768]{1,0:T(8,128)(2,1)S(1)} collective-permute-done((bf16[192,768]{1,0:T(8,128)(2,1)}, bf16[192,768]{1,0:T(8,128)(2,1)S(1)}, u32[]{:S(2)}, u32[]{:S(2)}) %collective-permute-start.29) | collective-permute-done | bytes 294944 | tf_op jit(solution)/shard_map/ppermute | solution.py:705
  280.7 9.0 %table_sums.3.table1_ref = f32[72,128]{1,0:T(8,128)} custom-call(f32[3,200,200]{2,1,0:T(8,128)} %get-tuple-element.195.refs_0_, f32[3,200,200]{2,1,0:T(8,128)} %get-tuple-element.196.refs_1_, f32[3,200,200]{2,1,0:T(8,128)} %get-tuple-element.197.refs_2_, f32[3,200,200]{2,1,0:T(8,128)} %get-tuple-element.198.refs_3_, s32[200,200]{1,0:T(8,128)} %bitcast.39), custom_call_target="tpu_custom_call" | custom-call | flops 880000000 | tf_op jit(solution)/shard_map/table_sums/pallas_call | solution.py:209
  292.3 8.0 %table_sums.2.table0_ref = f32[72,128]{1,0:T(8,128)} custom-call(f32[3,200,200]{2,1,0:T(8,128)} %get-tuple-element.195.refs_0_, f32[3,200,200]{2,1,0:T(8,128)} %get-tuple-element.196.refs_1_, f32[3,200,200]{2,1,0:T(8,128)} %get-tuple-element.197.refs_2_, f32[3,200,200]{2,1,0:T(8,128)} %get-tuple-element.198.refs_3_, s32[200,200]{1,0:T(8,128)} %bitcast.40), custom_call_target="tpu_custom_call" | custom-call | flops 880000000 | tf_op jit(solution)/shard_map/table_sums/pallas_call | solution.py:209
  312.5 6.5 %collective-permute-done.35.refs_1_ = bf16[96,768]{1,0:T(8,128)(2,1)S(1)} collective-permute-done((bf16[96,768]{1,0:T(8,128)(2,1)}, bf16[96,768]{1,0:T(8,128)(2,1)S(1)}, u32[]{:S(2)}, u32[]{:S(2)}) %collective-permute-start.35) | collective-permute-done | bytes 147488 | tf_op jit(solution)/shard_map/ppermute | solution.py:705
  325.2 7.4 %collective-permute-start.38 = (bf16[192,768]{1,0:T(8,128)(2,1)}, bf16[192,768]{1,0:T(8,128)(2,1)S(1)}, u32[]{:S(2)}, u32[]{:S(2)}) collective-permute-start(bf16[192,768]{1,0:T(8,128)(2,1)} %get-tuple-element.228.refs_2_), channel_id=1, source_target_pairs={{0,8},{4,12},{8,0},{12,4},{16,24},{20,28},{24,16},{28,20},{1,9},{5... | collective-permute-start | bytes 884744 | tf_op jit(solution)/shard_map/ppermute | solution.py:705
  332.7 4.3 %collective-permute-done.24 = f32[24,768]{1,0:T(8,128)S(1)} collective-permute-done((f32[24,768]{1,0:T(8,128)S(1)}, f32[24,768]{1,0:T(8,128)S(1)}, u32[]{:S(2)}, u32[]{:S(2)}) %collective-permute-start.24) | collective-permute-done | bytes 73760 | tf_op jit(solution)/shard_map/ppermute | solution.py:705
  338.4 12.4 %collective-permute-done.25 = f32[24,768]{1,0:T(8,128)S(1)} collective-permute-done((f32[24,768]{1,0:T(8,128)S(1)}, f32[24,768]{1,0:T(8,128)S(1)}, u32[]{:S(2)}, u32[]{:S(2)}) %collective-permute-start.25) | collective-permute-done | bytes 73760 | tf_op jit(solution)/shard_map/ppermute | solution.py:705
  353.0 4.0 %collective-permute-done.26.got_ref = f32[24,768]{1,0:T(8,128)S(1)} collective-permute-done((f32[24,768]{1,0:T(8,128)S(1)}, f32[24,768]{1,0:T(8,128)S(1)}, u32[]{:S(2)}, u32[]{:S(2)}) %collective-permute-start.26) | collective-permute-done | bytes 73760 | tf_op jit(solution)/shard_map/ppermute | solution.py:705
  (172 shorter events, 90.2 us)
Async XLA Ops:
  7.2 356.3 %all-reduce.4.cloned.1.call-start = ((), (), s32[]{:S(2)}) async-start(), calls=%async_computation | async-start | bytes 4718592 | tf_op jit(solution)/shard_map/psum | solution.py:1004
  13.1 21.6 %collective-permute-start = (bf16[576,768]{1,0:T(8,128)(2,1)S(1)}, bf16[576,768]{1,0:T(8,128)(2,1)}, u32[]{:S(2)}, u32[]{:S(2)}) collective-permute-start(bf16[576,768]{1,0:T(8,128)(2,1)S(1)} %bitcast.37), channel_id=1, source_target_pairs={{0,1},{1,0},{2,3},{3,2},{4,5},{5,4},{6,7},{7,6},{8,9},{9,8},{10,11... | collective-permute-start | bytes 2654216 | tf_op jit(solution)/shard_map/ppermute | solution.py:705
  27.2 27.0 %collective-permute-start.4 = (bf16[400,768]{1,0:T(8,128)(2,1)S(1)}, bf16[400,768]{1,0:T(8,128)(2,1)}, u32[]{:S(2)}, u32[]{:S(2)}) collective-permute-start(bf16[400,768]{1,0:T(8,128)(2,1)S(1)} %collective-permute-done.3.near_ref.p0_ref.s0_ref.refs_7_), channel_id=1, source_target_pairs={{0,4},{4,0},{8,12},{12,8},{16,20},{20,16},{24,28},{28,24},{1,5},{5... | collective-permute-start | bytes 1843208 | tf_op jit(solution)/shard_map/ppermute | solution.py:705
  28.9 25.3 %collective-permute-start.5 = (bf16[768,384]{1,0:T(8,128)(2,1)}, bf16[768,384]{1,0:T(8,128)(2,1)}, u32[]{:S(2)}, u32[]{:S(2)}) collective-permute-start(bf16[768,384]{1,0:T(8,128)(2,1)} %get-tuple-element.137), channel_id=1, source_target_pairs={{0,2},{1,3},{2,0},{3,1},{4,6},{5,7},{6,4},{7,5},{8,10},{9,11},{10,... | collective-permute-start | bytes 1769480 | tf_op jit(solution)/shard_map/ppermute | solution.py:705
  32.8 48.2 %collective-permute-start.8 = (bf16[768,768]{1,0:T(8,128)(2,1)S(1)}, bf16[768,768]{1,0:T(8,128)(2,1)}, u32[]{:S(2)}, u32[]{:S(2)}) collective-permute-start(bf16[768,768]{1,0:T(8,128)(2,1)S(1)} %copy-done.5), channel_id=1, source_target_pairs={{0,2},{1,3},{2,0},{3,1},{4,6},{5,7},{6,4},{7,5},{8,10},{9,11},{10,... | collective-permute-start | bytes 3538952 | tf_op jit(solution)/shard_map/ppermute | solution.py:705
  34.5 20.3 %collective-permute-start.6 = (bf16[400,768]{1,0:T(8,128)(2,1)S(1)}, bf16[400,768]{1,0:T(8,128)(2,1)S(1)}, u32[]{:S(2)}, u32[]{:S(2)}) collective-permute-start(bf16[400,768]{1,0:T(8,128)(2,1)S(1)} %collective-permute-done.3.near_ref.p0_ref.s0_ref.refs_7_), channel_id=1, source_target_pairs={{0,1},{1,0},{2,3},{3,2},{4,5},{5,4},{6,7},{7,6},{8,9},{9,8},{10,11... | collective-permute-start | bytes 1843208 | tf_op jit(solution)/shard_map/ppermute | solution.py:705
  54.5 26.5 %collective-permute-start.9 = (bf16[768,384]{1,0:T(8,128)(2,1)}, bf16[768,384]{1,0:T(8,128)(2,1)S(1)}, u32[]{:S(2)}, u32[]{:S(2)}) collective-permute-start(bf16[768,384]{1,0:T(8,128)(2,1)} %collective-permute-done.5.refs_5_), channel_id=1, source_target_pairs={{0,4},{4,0},{8,12},{12,8},{16,20},{20,16},{24,28},{28,24},{1,5},{5... | collective-permute-start | bytes 1769480 | tf_op jit(solution)/shard_map/ppermute | solution.py:705
  54.8 27.3 %collective-permute-start.13 = (bf16[768,768]{1,0:T(8,128)(2,1)S(1)}, bf16[768,768]{1,0:T(8,128)(2,1)S(1)}, u32[]{:S(2)}, u32[]{:S(2)}) collective-permute-start(bf16[768,768]{1,0:T(8,128)(2,1)S(1)} %copy-done.5), channel_id=1, source_target_pairs={{0,1},{1,0},{2,3},{3,2},{4,5},{5,4},{6,7},{7,6},{8,9},{9,8},{10,11... | collective-permute-start | bytes 3538952 | tf_op jit(solution)/shard_map/ppermute | solution.py:705
  54.8 27.2 %collective-permute-start.14 = (bf16[768,768]{1,0:T(8,128)(2,1)S(1)}, bf16[768,768]{1,0:T(8,128)(2,1)}, u32[]{:S(2)}, u32[]{:S(2)}) collective-permute-start(bf16[768,768]{1,0:T(8,128)(2,1)S(1)} %copy-done.2), channel_id=1, source_target_pairs={{0,1},{1,0},{2,3},{3,2},{4,5},{5,4},{6,7},{7,6},{8,9},{9,8},{10,11... | collective-permute-start | bytes 3538952 | tf_op jit(solution)/shard_map/ppermute | solution.py:705
  81.0 17.7 %collective-permute-start.10 = (bf16[768,768]{1,0:T(8,128)(2,1)}, bf16[768,768]{1,0:T(8,128)(2,1)S(1)}, u32[]{:S(2)}, u32[]{:S(2)}) collective-permute-start(bf16[768,768]{1,0:T(8,128)(2,1)} %collective-permute-done.8.refs_4_), channel_id=1, source_target_pairs={{0,1},{1,0},{2,3},{3,2},{4,5},{5,4},{6,7},{7,6},{8,9},{9,8},{10,11... | collective-permute-start | bytes 3538952 | tf_op jit(solution)/shard_map/ppermute | solution.py:705
  81.5 17.2 %collective-permute-start.11 = (bf16[768,384]{1,0:T(8,128)(2,1)}, bf16[768,384]{1,0:T(8,128)(2,1)S(1)}, u32[]{:S(2)}, u32[]{:S(2)}) collective-permute-start(bf16[768,384]{1,0:T(8,128)(2,1)} %collective-permute-done.5.refs_5_), channel_id=1, source_target_pairs={{0,1},{1,0},{2,3},{3,2},{4,5},{5,4},{6,7},{7,6},{8,9},{9,8},{10,11... | collective-permute-start | bytes 1769480 | tf_op jit(solution)/shard_map/ppermute | solution.py:705
  81.6 17.1 %collective-permute-start.12 = (bf16[768,384]{1,0:T(8,128)(2,1)S(1)}, bf16[768,384]{1,0:T(8,128)(2,1)S(1)}, u32[]{:S(2)}, u32[]{:S(2)}) collective-permute-start(bf16[768,384]{1,0:T(8,128)(2,1)S(1)} %collective-permute-done.9.refs_6_), channel_id=1, source_target_pairs={{0,1},{1,0},{2,3},{3,2},{4,5},{5,4},{6,7},{7,6},{8,9},{9,8},{10,11... | collective-permute-start | bytes 1769480 | tf_op jit(solution)/shard_map/ppermute | solution.py:705
  118.6 19.0 %collective-permute-start.15 = (bf16[768,768]{1,0:T(8,128)(2,1)}, bf16[768,768]{1,0:T(8,128)(2,1)S(1)}, u32[]{:S(2)}, u32[]{:S(2)}) collective-permute-start(bf16[768,768]{1,0:T(8,128)(2,1)} %get-tuple-element.152), channel_id=1, source_target_pairs={{0,1},{1,0},{2,3},{3,2},{4,5},{5,4},{6,7},{7,6},{8,9},{9,8},{10,11... | collective-permute-start | bytes 3538952 | tf_op jit(solution)/shard_map/ppermute | solution.py:705
  118.8 18.8 %collective-permute-start.16 = (bf16[768,768]{1,0:T(8,128)(2,1)}, bf16[768,768]{1,0:T(8,128)(2,1)S(1)}, u32[]{:S(2)}, u32[]{:S(2)}) collective-permute-start(bf16[768,768]{1,0:T(8,128)(2,1)} %get-tuple-element.158), channel_id=1, source_target_pairs={{0,1},{1,0},{2,3},{3,2},{4,5},{5,4},{6,7},{7,6},{8,9},{9,8},{10,11... | collective-permute-start | bytes 3538952 | tf_op jit(solution)/shard_map/ppermute | solution.py:705
  119.2 66.1 %collective-permute-start.17 = (bf16[768,768]{1,0:T(8,128)(2,1)}, bf16[768,768]{1,0:T(8,128)(2,1)S(1)}, u32[]{:S(2)}, u32[]{:S(2)}) collective-permute-start(bf16[768,768]{1,0:T(8,128)(2,1)} %get-tuple-element.172), channel_id=1, source_target_pairs={{0,1},{1,0},{2,3},{3,2},{4,5},{5,4},{6,7},{7,6},{8,9},{9,8},{10,11... | collective-permute-start | bytes 3538952 | tf_op jit(solution)/shard_map/ppermute | solution.py:705
  139.8 45.6 %collective-permute-start.18 = (bf16[768,768]{1,0:T(8,128)(2,1)S(1)}, bf16[768,768]{1,0:T(8,128)(2,1)S(1)}, u32[]{:S(2)}, u32[]{:S(2)}) collective-permute-start(bf16[768,768]{1,0:T(8,128)(2,1)S(1)} %get-tuple-element.173), channel_id=1, source_target_pairs={{0,2},{1,3},{2,0},{3,1},{4,6},{5,7},{6,4},{7,5},{8,10},{9,11},{10,... | collective-permute-start | bytes 3538952 | tf_op jit(solution)/shard_map/ppermute | solution.py:705
  141.6 45.2 %collective-permute-start.19 = (bf16[768,768]{1,0:T(8,128)(2,1)}, bf16[768,768]{1,0:T(8,128)(2,1)S(1)}, u32[]{:S(2)}, u32[]{:S(2)}) collective-permute-start(bf16[768,768]{1,0:T(8,128)(2,1)} %get-tuple-element.175), channel_id=1, source_target_pairs={{0,1},{1,0},{2,3},{3,2},{4,5},{5,4},{6,7},{7,6},{8,9},{9,8},{10,11... | collective-permute-start | bytes 3538952 | tf_op jit(solution)/shard_map/ppermute | solution.py:705
  159.3 34.3 %collective-permute-start.20 = (bf16[768,768]{1,0:T(8,128)(2,1)S(1)}, bf16[768,768]{1,0:T(8,128)(2,1)}, u32[]{:S(2)}, u32[]{:S(2)}) collective-permute-start(bf16[768,768]{1,0:T(8,128)(2,1)S(1)} %get-tuple-element.176), channel_id=1, source_target_pairs={{0,2},{1,3},{2,0},{3,1},{4,6},{5,7},{6,4},{7,5},{8,10},{9,11},{10,... | collective-permute-start | bytes 3538952 | tf_op jit(solution)/shard_map/ppermute | solution.py:705
  185.3 26.2 %collective-permute-start.21 = (bf16[768,768]{1,0:T(8,128)(2,1)}, bf16[768,768]{1,0:T(8,128)(2,1)S(1)}, u32[]{:S(2)}, u32[]{:S(2)}) collective-permute-start(bf16[768,768]{1,0:T(8,128)(2,1)} %get-tuple-element.183), channel_id=1, source_target_pairs={{0,1},{1,0},{2,3},{3,2},{4,5},{5,4},{6,7},{7,6},{8,9},{9,8},{10,11... | collective-permute-start | bytes 3538952 | tf_op jit(solution)/shard_map/ppermute | solution.py:705
  228.2 19.7 %collective-permute-start.27 = (bf16[768,768]{1,0:T(8,128)(2,1)}, bf16[768,768]{1,0:T(8,128)(2,1)S(1)}, u32[]{:S(2)}, u32[]{:S(2)}) collective-permute-start(bf16[768,768]{1,0:T(8,128)(2,1)} %get-tuple-element.213), channel_id=1, source_target_pairs={{0,1},{1,0},{2,3},{3,2},{4,5},{5,4},{6,7},{7,6},{8,9},{9,8},{10,11... | collective-permute-start | bytes 3538952 | tf_op jit(solution)/shard_map/ppermute | solution.py:705
  228.2 28.4 %collective-permute-start.28 = (bf16[768,768]{1,0:T(8,128)(2,1)S(1)}, bf16[768,768]{1,0:T(8,128)(2,1)S(1)}, u32[]{:S(2)}, u32[]{:S(2)}) collective-permute-start(bf16[768,768]{1,0:T(8,128)(2,1)S(1)} %add_convert_fusion), channel_id=1, source_target_pairs={{0,2},{1,3},{2,0},{3,1},{4,6},{5,7},{6,4},{7,5},{8,10},{9,11},{10,... | collective-permute-start | bytes 3538952 | tf_op jit(solution)/shard_map/ppermute | solution.py:705
  310.9 21.7 %collective-permute-start.23 = (f32[24,768]{1,0:T(8,128)S(1)}, f32[24,768]{1,0:T(8,128)S(1)}, u32[]{:S(2)}, u32[]{:S(2)}) collective-permute-start(f32[24,768]{1,0:T(8,128)S(1)} %pad_maximum_fusion), channel_id=1, source_target_pairs={{0,2},{1,3},{2,0},{3,1},{4,6},{5,7},{6,4},{7,5},{8,10},{9,11},{10,... | collective-permute-start | bytes 221192 | tf_op jit(solution)/shard_map/ppermute | solution.py:705
  322.2 37.0 %collective-permute-start.37 = (bf16[192,768]{1,0:T(8,128)(2,1)}, bf16[192,768]{1,0:T(8,128)(2,1)S(1)}, u32[]{:S(2)}, u32[]{:S(2)}) collective-permute-start(bf16[192,768]{1,0:T(8,128)(2,1)} %get-tuple-element.227.refs_0_), channel_id=1, source_target_pairs={{0,4},{4,0},{8,12},{12,8},{16,20},{20,16},{24,28},{28,24},{1,5},{5... | collective-permute-start | bytes 884744 | tf_op jit(solution)/shard_map/ppermute | solution.py:705
  325.2 34.0 %collective-permute-start.38 = (bf16[192,768]{1,0:T(8,128)(2,1)}, bf16[192,768]{1,0:T(8,128)(2,1)S(1)}, u32[]{:S(2)}, u32[]{:S(2)}) collective-permute-start(bf16[192,768]{1,0:T(8,128)(2,1)} %get-tuple-element.228.refs_2_), channel_id=1, source_target_pairs={{0,8},{4,12},{8,0},{12,4},{16,24},{20,28},{24,16},{28,20},{1,9},{5... | collective-permute-start | bytes 884744 | tf_op jit(solution)/shard_map/ppermute | solution.py:705
  (51 other events, 351.3 us)
Sparse Core Ops, SparseCore 0:
  230.1 119.6 all-reduce.3
